TPU v7x, 768 devices: a whole 4x8x12 slice. The times are simulated.
768 devices in a mesh: dp: 96 (over y, z), tensor: 8 (over x, core).
Axes of the slice: x: 4, y: 8, z: 12, core: 2. Of those that a mesh axis runs over, the one named last changes fastest.
Arguments:
- queries: bfloat16 [49152, 3072], P('dp', 'tensor'), may hold values from -6 to 6
- keys: bfloat16 [49152, 3072], P('dp', 'tensor'), may hold values from -6 to 6
- values: bfloat16 [49152, 3072], P('dp', 'tensor'), may hold values from -6 to 6
- out_grad: bfloat16 [49152, 3072], P('dp', 'tensor'), may hold values from -6 to 6
- lengths: int32 [384], replicated, may hold values from 1 to 512, 49152 in all
Outputs:
- attn_out: bfloat16 [49152, 3072], P('dp', 'tensor')
- query_grad: bfloat16 [49152, 3072], P('dp', 'tensor')
- key_grad: bfloat16 [49152, 3072], P('dp', 'tensor')
- value_grad: bfloat16 [49152, 3072], P('dp', 'tensor')
Inputs may be any that keep to these rules, and one draw needn't show every extreme that they name: `lengths`: 384 token counts that sum to 49152, at least one image 512 long.
All inputs are finite; a program needn't handle non-finite values.
Results may differ from a plain program's by a relative error of at most 0.012.
Values may be sent and summed in bfloat16 or wider, within the bound.
A program may use at most 64 MiB of HBM per device.

v0:
```python
import math

import jax
import jax.numpy as jnp
from jax import lax
from jax.sharding import PartitionSpec as P

HEAD_DIM = 128


def passed_along(value, axis, steps):
    count = lax.axis_size(axis)
    leading, last = (max(0, -steps), min(count, count - steps))
    return lax.ppermute(value, axis, [(source, source + steps) for source in range(leading, last)])


def image_masks(lengths, first_row, count, total_rows, span):
    ends = jnp.cumsum(lengths)
    starts = ends - lengths
    positions = first_row + jnp.arange(count, dtype=jnp.int32)
    begin = jnp.max(jnp.where(starts[None, :] <= positions[:, None], starts[None, :], -1), axis=1)
    valid = positions < total_rows
    owned_rows = valid & (begin >= first_row) & (begin < first_row + span)
    window_mask = owned_rows[:, None] & valid[None, :] & (begin[:, None] == begin[None, :])
    return (window_mask, owned_rows)


def head_attention(operands, window_mask, owned_rows, factor):
    query_head, key_head, value_head, grad_head = operands
    scores = jnp.dot(query_head, key_head.T, preferred_element_type=jnp.float32) * factor
    scores = jnp.where(window_mask, scores, -1e30)
    top_score = jnp.max(scores, axis=1, keepdims=True)
    weights = jnp.where(window_mask, jnp.exp(scores - top_score), 0.0)
    totals = jnp.sum(weights, axis=1, keepdims=True)
    totals = jnp.where(owned_rows[:, None], totals, 1.0)
    probs = weights / totals
    probs_low = probs.astype(jnp.bfloat16)
    result = jnp.dot(probs_low, value_head, preferred_element_type=jnp.float32).astype(jnp.bfloat16)
    grad_probs = jnp.dot(grad_head, value_head.T, preferred_element_type=jnp.float32)
    centre = jnp.sum(
        grad_head.astype(jnp.float32) * result.astype(jnp.float32), axis=1, keepdims=True
    )
    grad_scores = (probs * (grad_probs - centre)).astype(jnp.bfloat16)
    grad_query = (
        jnp.dot(grad_scores, key_head, preferred_element_type=jnp.float32) * factor
    ).astype(jnp.bfloat16)
    grad_key = (
        jnp.dot(grad_scores.T, query_head, preferred_element_type=jnp.float32) * factor
    ).astype(jnp.bfloat16)
    grad_value = jnp.dot(probs_low.T, grad_head, preferred_element_type=jnp.float32).astype(
        jnp.bfloat16
    )
    return (result, grad_query, grad_key, grad_value)


def all_heads(window, window_mask, owned_rows):
    count = window[0].shape[0]
    factor = 1.0 / math.sqrt(HEAD_DIM)

    def split_heads(block):
        return block.reshape(count, -1, HEAD_DIM).transpose(1, 0, 2)

    stacked = (
        split_heads(window[0]),
        split_heads(window[1]),
        split_heads(window[2]),
        split_heads(window[3]),
    )

    def one_head(operands):
        return head_attention(operands, window_mask, owned_rows, factor)

    outputs = lax.map(one_head, stacked)
    return tuple((output.transpose(1, 0, 2).reshape(count, -1) for output in outputs))


def body(queries, keys, values, out_grad, lengths):
    rows = queries.shape[0]
    first_row = lax.axis_index("dp") * rows
    total_rows = rows * lax.axis_size("dp")
    local = (queries, keys, values, out_grad)
    window_mask, owned_rows = image_masks(lengths, first_row, 2 * rows, total_rows, rows)
    beyond = passed_along((queries, keys, values, out_grad), "dp", -1)
    window = tuple(
        (
            jnp.concatenate([own_block, extra_block], axis=0)
            for own_block, extra_block in zip(local, beyond)
        )
    )
    results = all_heads(window, window_mask, owned_rows)
    returned = passed_along(
        (results[0][rows:], results[1][rows:], results[2][rows:], results[3][rows:]), "dp", 1
    )
    merged = tuple(
        (result_block[:rows] + back_block for result_block, back_block in zip(results, returned))
    )
    return (merged[0], merged[1], merged[2], merged[3])


def solution(mesh):
    in_specs = (P("dp", "tensor"), P("dp", "tensor"), P("dp", "tensor"), P("dp", "tensor"), P())
    out_specs = (P("dp", "tensor"), P("dp", "tensor"), P("dp", "tensor"), P("dp", "tensor"))
    return jax.shard_map(body, mesh=mesh, in_specs=in_specs, out_specs=out_specs, check_vma=False)
```

profile of v0, /device:TPU:38, one launch (start us, length us, event | category | flops | bytes accessed | tf_op | source)
XLA Modules:
  0.0 162.2 jit_solution(17836757138175591008)
XLA Ops:
  1.8 14.5 %collective-permute-start = (bf16[512,384]{0,1:T(8,128)(2,1)S(1)}, bf16[512,384]{0,1:T(8,128)(2,1)}, u32[]{:S(2)}, u32[]{:S(2)}) collective-permute-start(bf16[512,384]{0,1:T(8,128)(2,1)S(1)} %copy.45), channel_id=1, source_target_pairs={{8,0},{16,8},{24,16},{32,24},{40,32},{48,40},{56,48},{64,56},{72,6... | collective-permute-start | bytes 1179656 | tf_op jit(solution)/shard_map/ppermute | solution.py:14
  17.5 2.5 %collective-permute-start.1 = (bf16[512,384]{0,1:T(8,128)(2,1)S(1)}, bf16[512,384]{0,1:T(8,128)(2,1)S(1)}, u32[]{:S(2)}, u32[]{:S(2)}) collective-permute-start(bf16[512,384]{0,1:T(8,128)(2,1)S(1)} %copy.47), channel_id=1, source_target_pairs={{8,0},{16,8},{24,16},{32,24},{40,32},{48,40},{56,48},{64,56},{72,6... | collective-permute-start | bytes 1179656 | tf_op jit(solution)/shard_map/ppermute | solution.py:14
  21.1 2.5 %collective-permute-start.2 = (bf16[512,384]{0,1:T(8,128)(2,1)S(1)}, bf16[512,384]{0,1:T(8,128)(2,1)S(1)}, u32[]{:S(2)}, u32[]{:S(2)}) collective-permute-start(bf16[512,384]{0,1:T(8,128)(2,1)S(1)} %copy.49), channel_id=1, source_target_pairs={{8,0},{16,8},{24,16},{32,24},{40,32},{48,40},{56,48},{64,56},{72,6... | collective-permute-start | bytes 1179656 | tf_op jit(solution)/shard_map/ppermute | solution.py:14
  23.6 2.5 %collective-permute-start.3 = (bf16[512,384]{1,0:T(8,128)(2,1)}, bf16[512,384]{1,0:T(8,128)(2,1)S(1)}, u32[]{:S(2)}, u32[]{:S(2)}) collective-permute-start(bf16[512,384]{1,0:T(8,128)(2,1)} %param.10), channel_id=1, source_target_pairs={{8,0},{16,8},{24,16},{32,24},{40,32},{48,40},{56,48},{64,56},{72,6... | collective-permute-start | bytes 1179656 | tf_op jit(solution)/shard_map/ppermute | solution.py:14
  28.5 21.6 %collective-permute-done.3 = bf16[512,384]{1,0:T(8,128)(2,1)S(1)} collective-permute-done((bf16[512,384]{1,0:T(8,128)(2,1)}, bf16[512,384]{1,0:T(8,128)(2,1)S(1)}, u32[]{:S(2)}, u32[]{:S(2)}) %collective-permute-start.3) | collective-permute-done | bytes 393248 | tf_op jit(solution)/shard_map/ppermute | solution.py:14
  51.4 2.0 %pad_maximum_fusion = bf16[1024,384]{0,1:T(8,128)(2,1)} fusion(bf16[512,384]{0,1:T(8,128)(2,1)} %collective-permute-done, bf16[512,384]{0,1:T(8,128)(2,1)S(1)} %copy.45), kind=kLoop, calls=%fused_computation.49 | loop fusion | flops 1572864 | bytes 1572864 | tf_op jit(solution)/shard_map/concatenate | solution.py:86
  55.4 63.6 %while.18 = (s32[]{:T(128)}, bf16[3,1024,128]{1,2,0:T(8,128)(2,1)}, bf16[3,1024,128]{1,2,0:T(8,128)(2,1)}, bf16[3,1024,128]{1,2,0:T(8,128)(2,1)}, bf16[3,1024,12...) while((s32[]{:T(128)}, bf16[3,1024,128]{1,2,0:T(8,128)(2,1)}, ...), condition=%wide.region_7.8_spmd.clone.clone, body=%wide.region_3.7_spmd.clone.clone.sunk | while | flops 1640232960 | bytes 59572384 | solution.py:73
  55.4 2.7 %fusion.63 = (f32[1024]{0:T(1024)S(1)}, f32[1024,1024]{0,1:T(8,128)S(1)}) fusion(s32[1024]{0:T(1024)S(1)} %get-tuple-element.333, pred[1024]{0:T(1024)(128)(4,1)S(1)} %get-tuple-element.329, pred[1024]{0:T(1024)(128)(4,1)S(1)} %get-tuple-element.332, bf16[3,1024,128]{1,2,0:T(8,128)(2,1)} %get-tuple-element.328, s32[]{:T(128)} %get-tuple-element.309, ...), kind=kOutput, calls=%fused_computation.5.clone.1 | convolution fusion | flops 274725888 | bytes 4733952 | tf_op jit(solution)/shard_map/while/body/eval_jaxpr/dot_general | solution.py:30
  58.0 2.2 %fusion.64 = f32[1024]{0:T(1024)S(1)} fusion(f32[1024,1024]{0,1:T(8,128)S(1)} %get-tuple-element.290, s32[1024]{0:T(1024)S(1)} %get-tuple-element.333, f32[1024]{0:T(1024)S(1)} %get-tuple-element.291, pred[1024]{0:T(1024)(128)(4,1)S(1)} %get-tuple-element.329, pred[1024]{0:T(1024)(128)(4,1)S(1)} %get-tuple-element.332), kind=kLoop, calls=%fused_computation.7.clone.1 | loop fusion | flops 8387584 | bytes 4208640 | tf_op jit(solution)/shard_map/while/body/eval_jaxpr/reduce_sum | solution.py:34
  60.2 2.2 %fusion.65 = f32[1024,1024]{0,1:T(8,128)S(1)} fusion(f32[1024,1024]{0,1:T(8,128)S(1)} %get-tuple-element.290, s32[1024]{0:T(1024)S(1)} %get-tuple-element.333, f32[1024]{0:T(1024)S(1)} %broadcast_select_fusion.2, f32[1024]{0:T(1024)S(1)} %get-tuple-element.291, pred[1024]{0:T(1024)(128)(4,1)S(1)} %get-tuple-element.329, ...), kind=kLoop, calls=%fused_computation.6.clone.1 | loop fusion | flops 8388608 | bytes 8402944 | tf_op jit(solution)/shard_map/while/body/eval_jaxpr/div | solution.py:36
  62.4 2.3 %bitcast_dynamic-update-slice_fusion.2 = (bf16[3,1024,128]{1,2,0:T(8,128)(2,1)}, bf16[1024,128]{0,1:T(8,128)(2,1)S(1)}) fusion(bf16[3,1024,128]{1,2,0:T(8,128)(2,1)} %get-tuple-element.310, s32[]{:T(128)} %get-tuple-element.309, f32[1024,1024]{0,1:T(8,128)S(1)} %fusion.65, bf16[3,1024,128]{1,2,0:T(8,128)(2,1)} %get-tuple-element.330), kind=kOutput, calls=%fused_computation.29.clone.1 | convolution fusion | flops 269615104 | bytes 4981760 | tf_op jit(solution)/shard_map/while/body/eval_jaxpr/dot_general | solution.py:38
  68.4 2.9 %fusion.67 = bf16[1,1024,128]{2,1,0:T(8,128)(2,1)S(1)} fusion(f32[1024,1024]{0,1:T(8,128)} %copy-done, bf16[3,1024,128]{1,2,0:T(8,128)(2,1)S(1)} %get-tuple-element.331, s32[]{:T(128)} %get-tuple-element.309), kind=kOutput, calls=%fused_computation.16.clone.1 | convolution fusion | flops 269615104 | bytes 4718596 | tf_op jit(solution)/shard_map/while/body/eval_jaxpr/dot_general | solution.py:50
  72.1 1.8 %constant_dynamic-update-slice_fusion.6 = (bf16[3,1024,128]{1,2,0:T(8,128)(2,1)}, bf16[3,1024,128]{1,2,0:T(8,128)(2,1)}) fusion(bf16[3,1024,128]{1,2,0:T(8,128)(2,1)} %get-tuple-element.313, bf16[1,1024,128]{1,2,0:T(8,128)(2,1)} %copy.78, s32[]{:T(128)} %get-tuple-element.309, bf16[3,1024,128]{1,2,0:T(8,128)(2,1)} %get-tuple-element.312, ...), kind=kLoop, calls=%fused_computation.40.clone.1 | loop fusion | bytes 1049088 | tf_op jit(solution)/shard_map/while/body/jit(dynamic_update_index_in_dim)/dynamic_update_slice | solution.py:73
  76.5 2.7 %fusion.63 = (f32[1024]{0:T(1024)S(1)}, f32[1024,1024]{0,1:T(8,128)S(1)}) fusion(s32[1024]{0:T(1024)S(1)} %get-tuple-element.333, pred[1024]{0:T(1024)(128)(4,1)S(1)} %get-tuple-element.329, pred[1024]{0:T(1024)(128)(4,1)S(1)} %get-tuple-element.332, bf16[3,1024,128]{1,2,0:T(8,128)(2,1)} %get-tuple-element.328, s32[]{:T(128)} %get-tuple-element.309, ...), kind=kOutput, calls=%fused_computation.5.clone.1 | convolution fusion | flops 274725888 | bytes 4733952 | tf_op jit(solution)/shard_map/while/body/eval_jaxpr/dot_general | solution.py:30
  79.2 2.2 %fusion.64 = f32[1024]{0:T(1024)S(1)} fusion(f32[1024,1024]{0,1:T(8,128)S(1)} %get-tuple-element.290, s32[1024]{0:T(1024)S(1)} %get-tuple-element.333, f32[1024]{0:T(1024)S(1)} %get-tuple-element.291, pred[1024]{0:T(1024)(128)(4,1)S(1)} %get-tuple-element.329, pred[1024]{0:T(1024)(128)(4,1)S(1)} %get-tuple-element.332), kind=kLoop, calls=%fused_computation.7.clone.1 | loop fusion | flops 8387584 | bytes 4208640 | tf_op jit(solution)/shard_map/while/body/eval_jaxpr/reduce_sum | solution.py:34
  81.4 2.2 %fusion.65 = f32[1024,1024]{0,1:T(8,128)S(1)} fusion(f32[1024,1024]{0,1:T(8,128)S(1)} %get-tuple-element.290, s32[1024]{0:T(1024)S(1)} %get-tuple-element.333, f32[1024]{0:T(1024)S(1)} %broadcast_select_fusion.2, f32[1024]{0:T(1024)S(1)} %get-tuple-element.291, pred[1024]{0:T(1024)(128)(4,1)S(1)} %get-tuple-element.329, ...), kind=kLoop, calls=%fused_computation.6.clone.1 | loop fusion | flops 8388608 | bytes 8402944 | tf_op jit(solution)/shard_map/while/body/eval_jaxpr/div | solution.py:36
  83.6 2.3 %bitcast_dynamic-update-slice_fusion.2 = (bf16[3,1024,128]{1,2,0:T(8,128)(2,1)}, bf16[1024,128]{0,1:T(8,128)(2,1)S(1)}) fusion(bf16[3,1024,128]{1,2,0:T(8,128)(2,1)} %get-tuple-element.310, s32[]{:T(128)} %get-tuple-element.309, f32[1024,1024]{0,1:T(8,128)S(1)} %fusion.65, bf16[3,1024,128]{1,2,0:T(8,128)(2,1)} %get-tuple-element.330), kind=kOutput, calls=%fused_computation.29.clone.1 | convolution fusion | flops 269615104 | bytes 4981760 | tf_op jit(solution)/shard_map/while/body/eval_jaxpr/dot_general | solution.py:38
  89.6 2.9 %fusion.67 = bf16[1,1024,128]{2,1,0:T(8,128)(2,1)S(1)} fusion(f32[1024,1024]{0,1:T(8,128)} %copy-done, bf16[3,1024,128]{1,2,0:T(8,128)(2,1)S(1)} %get-tuple-element.331, s32[]{:T(128)} %get-tuple-element.309), kind=kOutput, calls=%fused_computation.16.clone.1 | convolution fusion | flops 269615104 | bytes 4718596 | tf_op jit(solution)/shard_map/while/body/eval_jaxpr/dot_general | solution.py:50
  93.3 1.8 %constant_dynamic-update-slice_fusion.6 = (bf16[3,1024,128]{1,2,0:T(8,128)(2,1)}, bf16[3,1024,128]{1,2,0:T(8,128)(2,1)}) fusion(bf16[3,1024,128]{1,2,0:T(8,128)(2,1)} %get-tuple-element.313, bf16[1,1024,128]{1,2,0:T(8,128)(2,1)} %copy.78, s32[]{:T(128)} %get-tuple-element.309, bf16[3,1024,128]{1,2,0:T(8,128)(2,1)} %get-tuple-element.312, ...), kind=kLoop, calls=%fused_computation.40.clone.1 | loop fusion | bytes 1049088 | tf_op jit(solution)/shard_map/while/body/jit(dynamic_update_index_in_dim)/dynamic_update_slice | solution.py:73
  97.7 2.7 %fusion.63 = (f32[1024]{0:T(1024)S(1)}, f32[1024,1024]{0,1:T(8,128)S(1)}) fusion(s32[1024]{0:T(1024)S(1)} %get-tuple-element.333, pred[1024]{0:T(1024)(128)(4,1)S(1)} %get-tuple-element.329, pred[1024]{0:T(1024)(128)(4,1)S(1)} %get-tuple-element.332, bf16[3,1024,128]{1,2,0:T(8,128)(2,1)} %get-tuple-element.328, s32[]{:T(128)} %get-tuple-element.309, ...), kind=kOutput, calls=%fused_computation.5.clone.1 | convolution fusion | flops 274725888 | bytes 4733952 | tf_op jit(solution)/shard_map/while/body/eval_jaxpr/dot_general | solution.py:30
  100.4 2.2 %fusion.64 = f32[1024]{0:T(1024)S(1)} fusion(f32[1024,1024]{0,1:T(8,128)S(1)} %get-tuple-element.290, s32[1024]{0:T(1024)S(1)} %get-tuple-element.333, f32[1024]{0:T(1024)S(1)} %get-tuple-element.291, pred[1024]{0:T(1024)(128)(4,1)S(1)} %get-tuple-element.329, pred[1024]{0:T(1024)(128)(4,1)S(1)} %get-tuple-element.332), kind=kLoop, calls=%fused_computation.7.clone.1 | loop fusion | flops 8387584 | bytes 4208640 | tf_op jit(solution)/shard_map/while/body/eval_jaxpr/reduce_sum | solution.py:34
  102.6 2.2 %fusion.65 = f32[1024,1024]{0,1:T(8,128)S(1)} fusion(f32[1024,1024]{0,1:T(8,128)S(1)} %get-tuple-element.290, s32[1024]{0:T(1024)S(1)} %get-tuple-element.333, f32[1024]{0:T(1024)S(1)} %broadcast_select_fusion.2, f32[1024]{0:T(1024)S(1)} %get-tuple-element.291, pred[1024]{0:T(1024)(128)(4,1)S(1)} %get-tuple-element.329, ...), kind=kLoop, calls=%fused_computation.6.clone.1 | loop fusion | flops 8388608 | bytes 8402944 | tf_op jit(solution)/shard_map/while/body/eval_jaxpr/div | solution.py:36
  104.8 2.3 %bitcast_dynamic-update-slice_fusion.2 = (bf16[3,1024,128]{1,2,0:T(8,128)(2,1)}, bf16[1024,128]{0,1:T(8,128)(2,1)S(1)}) fusion(bf16[3,1024,128]{1,2,0:T(8,128)(2,1)} %get-tuple-element.310, s32[]{:T(128)} %get-tuple-element.309, f32[1024,1024]{0,1:T(8,128)S(1)} %fusion.65, bf16[3,1024,128]{1,2,0:T(8,128)(2,1)} %get-tuple-element.330), kind=kOutput, calls=%fused_computation.29.clone.1 | convolution fusion | flops 269615104 | bytes 4981760 | tf_op jit(solution)/shard_map/while/body/eval_jaxpr/dot_general | solution.py:38
  110.7 2.9 %fusion.67 = bf16[1,1024,128]{2,1,0:T(8,128)(2,1)S(1)} fusion(f32[1024,1024]{0,1:T(8,128)} %copy-done, bf16[3,1024,128]{1,2,0:T(8,128)(2,1)S(1)} %get-tuple-element.331, s32[]{:T(128)} %get-tuple-element.309), kind=kOutput, calls=%fused_computation.16.clone.1 | convolution fusion | flops 269615104 | bytes 4718596 | tf_op jit(solution)/shard_map/while/body/eval_jaxpr/dot_general | solution.py:50
  120.1 1.9 %collective-permute-start.7 = (bf16[512,384]{0,1:T(8,128)(2,1)S(1)}, bf16[512,384]{0,1:T(8,128)(2,1)S(1)}, u32[]{:S(2)}, u32[]{:S(2)}) collective-permute-start(bf16[512,384]{0,1:T(8,128)(2,1)S(1)} %bitcast.111), channel_id=1, source_target_pairs={{0,8},{8,16},{16,24},{24,32},{32,40},{40,48},{48,56},{56,64},{64,7... | collective-permute-start | bytes 1179656 | tf_op jit(solution)/shard_map/ppermute | solution.py:14
  123.2 1.9 %collective-permute-start.6 = (bf16[512,384]{0,1:T(8,128)(2,1)S(1)}, bf16[512,384]{0,1:T(8,128)(2,1)}, u32[]{:S(2)}, u32[]{:S(2)}) collective-permute-start(bf16[512,384]{0,1:T(8,128)(2,1)S(1)} %bitcast.110), channel_id=1, source_target_pairs={{0,8},{8,16},{16,24},{24,32},{32,40},{40,48},{48,56},{56,64},{64,7... | collective-permute-start | bytes 1179656 | tf_op jit(solution)/shard_map/ppermute | solution.py:14
  126.3 1.9 %collective-permute-start.5 = (bf16[512,384]{0,1:T(8,128)(2,1)S(1)}, bf16[512,384]{0,1:T(8,128)(2,1)S(1)}, u32[]{:S(2)}, u32[]{:S(2)}) collective-permute-start(bf16[512,384]{0,1:T(8,128)(2,1)S(1)} %bitcast.109), channel_id=1, source_target_pairs={{0,8},{8,16},{16,24},{24,32},{32,40},{40,48},{48,56},{56,64},{64,7... | collective-permute-start | bytes 1179656 | tf_op jit(solution)/shard_map/ppermute | solution.py:14
  129.4 3.0 %collective-permute-start.4 = (bf16[512,384]{0,1:T(8,128)(2,1)S(1)}, bf16[512,384]{0,1:T(8,128)(2,1)S(1)}, u32[]{:S(2)}, u32[]{:S(2)}) collective-permute-start(bf16[512,384]{0,1:T(8,128)(2,1)S(1)} %bitcast.108), channel_id=1, source_target_pairs={{0,8},{8,16},{16,24},{24,32},{32,40},{40,48},{48,56},{56,64},{64,7... | collective-permute-start | bytes 1179656 | tf_op jit(solution)/shard_map/ppermute | solution.py:14
  132.4 5.3 %collective-permute-done.7 = bf16[512,384]{0,1:T(8,128)(2,1)S(1)} collective-permute-done((bf16[512,384]{0,1:T(8,128)(2,1)S(1)}, bf16[512,384]{0,1:T(8,128)(2,1)S(1)}, u32[]{:S(2)}, u32[]{:S(2)}) %collective-permute-start.7) | collective-permute-done | bytes 393248 | tf_op jit(solution)/shard_map/ppermute | solution.py:14
  138.7 7.5 %collective-permute-done.6 = bf16[512,384]{0,1:T(8,128)(2,1)} collective-permute-done((bf16[512,384]{0,1:T(8,128)(2,1)S(1)}, bf16[512,384]{0,1:T(8,128)(2,1)}, u32[]{:S(2)}, u32[]{:S(2)}) %collective-permute-start.6) | collective-permute-done | bytes 393248 | tf_op jit(solution)/shard_map/ppermute | solution.py:14
  148.2 6.4 %collective-permute-done.5 = bf16[512,384]{0,1:T(8,128)(2,1)S(1)} collective-permute-done((bf16[512,384]{0,1:T(8,128)(2,1)S(1)}, bf16[512,384]{0,1:T(8,128)(2,1)S(1)}, u32[]{:S(2)}, u32[]{:S(2)}) %collective-permute-start.5) | collective-permute-done | bytes 393248 | tf_op jit(solution)/shard_map/ppermute | solution.py:14
  155.6 5.6 %collective-permute-done.4 = bf16[512,384]{0,1:T(8,128)(2,1)S(1)} collective-permute-done((bf16[512,384]{0,1:T(8,128)(2,1)S(1)}, bf16[512,384]{0,1:T(8,128)(2,1)S(1)}, u32[]{:S(2)}, u32[]{:S(2)}) %collective-permute-start.4) | collective-permute-done | bytes 393248 | tf_op jit(solution)/shard_map/ppermute | solution.py:14
  (68 shorter events, 41.7 us)
Async XLA Ops:
  1.8 49.6 %collective-permute-start = (bf16[512,384]{0,1:T(8,128)(2,1)S(1)}, bf16[512,384]{0,1:T(8,128)(2,1)}, u32[]{:S(2)}, u32[]{:S(2)}) collective-permute-start(bf16[512,384]{0,1:T(8,128)(2,1)S(1)} %copy.45), channel_id=1, source_target_pairs={{8,0},{16,8},{24,16},{32,24},{40,32},{48,40},{56,48},{64,56},{72,6... | collective-permute-start | bytes 1179656 | tf_op jit(solution)/shard_map/ppermute | solution.py:14
  17.5 35.9 %collective-permute-start.1 = (bf16[512,384]{0,1:T(8,128)(2,1)S(1)}, bf16[512,384]{0,1:T(8,128)(2,1)S(1)}, u32[]{:S(2)}, u32[]{:S(2)}) collective-permute-start(bf16[512,384]{0,1:T(8,128)(2,1)S(1)} %copy.47), channel_id=1, source_target_pairs={{8,0},{16,8},{24,16},{32,24},{40,32},{48,40},{56,48},{64,56},{72,6... | collective-permute-start | bytes 1179656 | tf_op jit(solution)/shard_map/ppermute | solution.py:14
  21.1 33.3 %collective-permute-start.2 = (bf16[512,384]{0,1:T(8,128)(2,1)S(1)}, bf16[512,384]{0,1:T(8,128)(2,1)S(1)}, u32[]{:S(2)}, u32[]{:S(2)}) collective-permute-start(bf16[512,384]{0,1:T(8,128)(2,1)S(1)} %copy.49), channel_id=1, source_target_pairs={{8,0},{16,8},{24,16},{32,24},{40,32},{48,40},{56,48},{64,56},{72,6... | collective-permute-start | bytes 1179656 | tf_op jit(solution)/shard_map/ppermute | solution.py:14
  23.6 26.4 %collective-permute-start.3 = (bf16[512,384]{1,0:T(8,128)(2,1)}, bf16[512,384]{1,0:T(8,128)(2,1)S(1)}, u32[]{:S(2)}, u32[]{:S(2)}) collective-permute-start(bf16[512,384]{1,0:T(8,128)(2,1)} %param.10), channel_id=1, source_target_pairs={{8,0},{16,8},{24,16},{32,24},{40,32},{48,40},{56,48},{64,56},{72,6... | collective-permute-start | bytes 1179656 | tf_op jit(solution)/shard_map/ppermute | solution.py:14
  62.4 4.1 %copy-start = (f32[1024,1024]{0,1:T(8,128)}, f32[1024,1024]{0,1:T(8,128)S(1)}, u32[]{:S(2)}) copy-start(f32[1024,1024]{0,1:T(8,128)S(1)} %fusion.65) | copy-start | bytes 12582916 | tf_op jit(solution)/shard_map/while
  83.6 4.1 %copy-start = (f32[1024,1024]{0,1:T(8,128)}, f32[1024,1024]{0,1:T(8,128)S(1)}, u32[]{:S(2)}) copy-start(f32[1024,1024]{0,1:T(8,128)S(1)} %fusion.65) | copy-start | bytes 12582916 | tf_op jit(solution)/shard_map/while
  104.8 4.1 %copy-start = (f32[1024,1024]{0,1:T(8,128)}, f32[1024,1024]{0,1:T(8,128)S(1)}, u32[]{:S(2)}) copy-start(f32[1024,1024]{0,1:T(8,128)S(1)} %fusion.65) | copy-start | bytes 12582916 | tf_op jit(solution)/shard_map/while
  120.1 17.6 %collective-permute-start.7 = (bf16[512,384]{0,1:T(8,128)(2,1)S(1)}, bf16[512,384]{0,1:T(8,128)(2,1)S(1)}, u32[]{:S(2)}, u32[]{:S(2)}) collective-permute-start(bf16[512,384]{0,1:T(8,128)(2,1)S(1)} %bitcast.111), channel_id=1, source_target_pairs={{0,8},{8,16},{16,24},{24,32},{32,40},{40,48},{48,56},{56,64},{64,7... | collective-permute-start | bytes 1179656 | tf_op jit(solution)/shard_map/ppermute | solution.py:14
  123.2 23.1 %collective-permute-start.6 = (bf16[512,384]{0,1:T(8,128)(2,1)S(1)}, bf16[512,384]{0,1:T(8,128)(2,1)}, u32[]{:S(2)}, u32[]{:S(2)}) collective-permute-start(bf16[512,384]{0,1:T(8,128)(2,1)S(1)} %bitcast.110), channel_id=1, source_target_pairs={{0,8},{8,16},{16,24},{24,32},{32,40},{40,48},{48,56},{56,64},{64,7... | collective-permute-start | bytes 1179656 | tf_op jit(solution)/shard_map/ppermute | solution.py:14
  126.3 28.3 %collective-permute-start.5 = (bf16[512,384]{0,1:T(8,128)(2,1)S(1)}, bf16[512,384]{0,1:T(8,128)(2,1)S(1)}, u32[]{:S(2)}, u32[]{:S(2)}) collective-permute-start(bf16[512,384]{0,1:T(8,128)(2,1)S(1)} %bitcast.109), channel_id=1, source_target_pairs={{0,8},{8,16},{16,24},{24,32},{32,40},{40,48},{48,56},{56,64},{64,7... | collective-permute-start | bytes 1179656 | tf_op jit(solution)/shard_map/ppermute | solution.py:14
  129.4 31.8 %collective-permute-start.4 = (bf16[512,384]{0,1:T(8,128)(2,1)S(1)}, bf16[512,384]{0,1:T(8,128)(2,1)S(1)}, u32[]{:S(2)}, u32[]{:S(2)}) collective-permute-start(bf16[512,384]{0,1:T(8,128)(2,1)S(1)} %bitcast.108), channel_id=1, source_target_pairs={{0,8},{8,16},{16,24},{24,32},{32,40},{40,48},{48,56},{56,64},{64,7... | collective-permute-start | bytes 1179656 | tf_op jit(solution)/shard_map/ppermute | solution.py:14
where the time goes:
time: 164 us; the launch traced here: 162 us
  waiting for transfers between devices  46.4 us (28%)
  matrix products  38.9 us (24%)
  starting transfers between devices  30.6 us (19%)
  local copies, waits for them, and re-layouts  23.4 us (14%)
  other arithmetic  21.8 us (13%)
    ppermute x8, waiting for transfers between devices, passed_along(): lax.ppermute(value, axis, [(source, source + steps) for source in range(l...  46.4 us
    ppermute x8, starting transfers between devices, passed_along(): lax.ppermute(value, axis, [(source, source + steps) for source in range(l...  30.6 us
    dynamic_update_slice x15, local copies, waits for them, and re-layouts, all_heads(): outputs = lax.map(one_head, stacked)  11 us
    dot_general x3, matrix products, head_attention(): jnp.dot(probs_low.T, grad_head, preferred_element_type=jnp.float32)  8.74 us
    dot_general x3, matrix products, head_attention(): jnp.dot(query_head, key_head.T, preferred_element_type=jnp.float32) * factor  8 us
    unnamed x7, local copies, waits for them, and re-layouts  7.18 us
    dot_general x3, matrix products, head_attention(): jnp.dot(probs_low, value_head, preferred_element_type=jnp.float32)  6.98 us
    div x3, other arithmetic, head_attention(): probs = weights / totals  6.55 us
  transfers between devices with their start and end apart: 8, of which 5 were waited for; matrix products, arithmetic and copies ran while one was open for 10% of the time, Pallas kernels for 0%

commit v1 on v0

v1 whole, which is shorter than its diff:
```python
import functools
import math

import jax
import jax.numpy as jnp
from jax import lax
from jax.experimental import pallas as pl
from jax.experimental.pallas import tpu as pltpu
from jax.sharding import PartitionSpec as P

D = 128
HALO = 256
BLK = 256
MESH = pl.DeviceIdType.MESH
LOG2E = 1.4426950408889634


def row_tables(len_ref, first, total, halo, rows):
    lens = len_ref[...]
    groups = lens.shape[0]
    upper = (
        lax.broadcasted_iota(jnp.int32, (128, 128), 0)
        <= lax.broadcasted_iota(jnp.int32, (128, 128), 1)
    ).astype(jnp.float32).astype(jnp.bfloat16)
    high = (lens >> 4).astype(jnp.float32).astype(jnp.bfloat16)
    low = (lens & 15).astype(jnp.float32).astype(jnp.bfloat16)
    within = 16.0 * jnp.dot(high, upper, preferred_element_type=jnp.float32) + jnp.dot(
        low, upper, preferred_element_type=jnp.float32
    )
    ends, base = [], jnp.zeros((1, 1), jnp.float32)
    for g in range(groups):
        ends.append(within[g : g + 1, :] + base)
        base = base + within[g : g + 1, 127:128]
    count = rows + 2 * halo
    pos = (
        first - halo + lax.broadcasted_iota(jnp.int32, (count, 128), 0)
    ).astype(jnp.float32)
    begin = jnp.full((count, 128), 0.0, jnp.float32)
    end = jnp.full((count, 128), 1e9, jnp.float32)
    for e in ends:
        past = e <= pos
        begin = jnp.maximum(begin, jnp.where(past, e, 0.0))
        end = jnp.minimum(end, jnp.where(past, 1e9, e))
    begin = jnp.max(begin, axis=1, keepdims=True)
    end = jnp.min(end, axis=1, keepdims=True)
    begin = jnp.where(pos[:, :1] < 0.0, -1.0, begin)
    return begin, end


def kernel(
    n_dp, rows, heads,
    q_hbm, k_hbm, v_hbm, g_hbm, len_ref,
    o_ref, dq_ref, dk_ref, dv_ref,
    win, res, from_left, from_right, idc, idr, qt, gt, p_s, ds_s,
    own_sem, send1, recv1, send2, recv2,
):
    halo, d = HALO, D
    count = rows + 2 * halo
    me = lax.axis_index("dp")
    ten = lax.axis_index("tensor")
    right = lax.rem(me + 1, n_dp)
    left = lax.rem(me + n_dp - 1, n_dp)
    srcs = (q_hbm, k_hbm, v_hbm, g_hbm)
    outs = (o_ref, dq_ref, dk_ref, dv_ref)

    def out_copy(x, h, way):
        cols = pl.ds(h * d, d)
        if way == 0:
            src, dst, who = pl.ds(rows - halo, halo), pl.ds(0, halo), right
        else:
            src, dst, who = pl.ds(0, halo), pl.ds(halo + rows, halo), left
        return pltpu.make_async_remote_copy(
            src_ref=srcs[x].at[src, cols],
            dst_ref=win.at[x, h, dst, :],
            send_sem=send1.at[h, x, way],
            recv_sem=recv1.at[h, x, way],
            device_id=(who, ten),
            device_id_type=MESH,
        )

    def back_copy(h, way):
        if way == 0:
            src, dst, who = res.at[:, h, pl.ds(halo + rows, halo), :], from_left.at[h], right
        else:
            src, dst, who = res.at[:, h, pl.ds(0, halo), :], from_right.at[h], left
        return pltpu.make_async_remote_copy(
            src_ref=src,
            dst_ref=dst,
            send_sem=send2.at[h, way],
            recv_sem=recv2.at[h, way],
            device_id=(who, ten),
            device_id_type=MESH,
        )

    def own_copy(x, h):
        return pltpu.make_async_copy(
            srcs[x].at[:, pl.ds(h * d, d)], win.at[x, h, pl.ds(halo, rows), :], own_sem.at[h, x]
        )

    barrier = pltpu.get_barrier_semaphore()
    for who in (left, right):
        pl.semaphore_signal(barrier, inc=1, device_id=(who, ten), device_id_type=MESH)
    pl.semaphore_wait(barrier, 2)

    for h in range(heads):
        for x in range(4):
            for way in range(2):
                out_copy(x, h, way).start()
    for h in range(heads):
        for x in range(4):
            own_copy(x, h).start()

    first = me * rows
    begin, end = row_tables(len_ref, first, rows * n_dp, halo, rows)
    idc[...] = jnp.broadcast_to(begin, (count, d))
    idr[...] = jnp.transpose(jnp.broadcast_to(begin, (count, d)))[:8, :]
    edge_l = first.astype(jnp.float32)
    edge_r = (first + rows).astype(jnp.float32)
    b_l, e_l = begin[halo : 2 * halo], end[halo : 2 * halo]
    gone_l = (b_l < edge_l) & (e_l - edge_l <= edge_l - b_l)
    b_r, e_r = begin[rows : rows + halo], end[rows : rows + halo]
    gone_r = (e_r > edge_r) & (e_r - edge_r > edge_r - b_r)
    factor = 1.0 / math.sqrt(d)
    nblk = count // BLK

    def one_head(h, carry):
        for x in range(4):
            own_copy(x, h).wait()
            for way in range(2):
                out_copy(x, h, way).wait_recv()
        qt[...] = jnp.transpose(win[0, h])
        gt[...] = jnp.transpose(win[3, h])
        for i in range(nblk):
            rs = slice(i * BLK, (i + 1) * BLK)
            ks = slice(max(0, i - 2) * BLK, min(nblk, i + 3) * BLK)
            qb, gb = win[0, h, rs, :], win[3, h, rs, :]
            kb, vb = win[1, h, ks, :], win[2, h, ks, :]
            s = lax.dot_general(
                qb, kb, (((1,), (1,)), ((), ())), preferred_element_type=jnp.float32
            ) * (factor * LOG2E)
            s = jnp.where(idc[rs, :1] == idr[:1, ks], s, -1e30)
            top = jnp.max(s, axis=1, keepdims=True)
            w = jnp.exp2(s - top)
            total = jnp.sum(w, axis=1, keepdims=True)
            probs = w * (1.0 / total)
            low = probs.astype(jnp.bfloat16)
            o = jnp.dot(low, vb, preferred_element_type=jnp.float32).astype(jnp.bfloat16)
            res[0, h, rs, :] = o
            p_s[rs, ks] = low
            gp = lax.dot_general(
                gb, vb, (((1,), (1,)), ((), ())), preferred_element_type=jnp.float32
            )
            centre = jnp.sum(
                gb.astype(jnp.float32) * o.astype(jnp.float32), axis=1, keepdims=True
            )
            ds = (probs * (gp - centre)).astype(jnp.bfloat16)
            ds_s[rs, ks] = ds
            res[1, h, rs, :] = (
                jnp.dot(ds, kb, preferred_element_type=jnp.float32) * factor
            ).astype(jnp.bfloat16)
        for j in range(nblk):
            js = slice(j * BLK, (j + 1) * BLK)
            rs = slice(max(0, j - 2) * BLK, min(nblk, j + 3) * BLK)
            dkt = jnp.dot(qt[:, rs], ds_s[rs, js], preferred_element_type=jnp.float32)
            dvt = jnp.dot(gt[:, rs], p_s[rs, js], preferred_element_type=jnp.float32)
            res[2, h, js, :] = jnp.transpose(dkt * factor).astype(jnp.bfloat16)
            res[3, h, js, :] = jnp.transpose(dvt).astype(jnp.bfloat16)
        for way in range(2):
            back_copy(h, way).start()
        return carry

    lax.fori_loop(0, heads, one_head, 0)

    for h in range(heads):
        for way in range(2):
            back_copy(h, way).wait_recv()
        cols = slice(h * d, (h + 1) * d)
        for x in range(4):
            outs[x][0:halo, cols] = jnp.where(
                gone_l, from_left[h, x], res[x, h, halo : 2 * halo, :]
            )
            outs[x][rows - halo : rows, cols] = jnp.where(
                gone_r, from_right[h, x], res[x, h, rows : rows + halo, :]
            )
    for h in range(heads):
        for way in range(2):
            back_copy(h, way).wait_send()
            for x in range(4):
                out_copy(x, h, way).wait_send()


def body(queries, keys, values, out_grad, lengths):
    rows, width = queries.shape
    heads = width // D
    n_dp = lax.axis_size("dp")
    count = rows + 2 * HALO
    out = jax.ShapeDtypeStruct((rows, width), jnp.bfloat16)
    bf = jnp.bfloat16
    pairs = count * count * heads
    return pl.pallas_call(
        functools.partial(kernel, n_dp, rows, heads),
        out_shape=(out,) * 4,
        in_specs=[pl.BlockSpec(memory_space=pl.ANY)] * 4 + [pl.BlockSpec(memory_space=pltpu.VMEM)],
        out_specs=(pl.BlockSpec(memory_space=pltpu.VMEM),) * 4,
        scratch_shapes=[
            pltpu.VMEM((4, heads, count, D), bf),
            pltpu.VMEM((4, heads, count, D), bf),
            pltpu.VMEM((heads, 4, HALO, D), bf),
            pltpu.VMEM((heads, 4, HALO, D), bf),
            pltpu.VMEM((count, D), jnp.float32),
            pltpu.VMEM((8, count), jnp.float32),
            pltpu.VMEM((D, count), bf),
            pltpu.VMEM((D, count), bf),
            pltpu.VMEM((count, count), bf),
            pltpu.VMEM((count, count), bf),
            pltpu.SemaphoreType.DMA((heads, 4)),
            pltpu.SemaphoreType.DMA((heads, 4, 2)),
            pltpu.SemaphoreType.DMA((heads, 4, 2)),
            pltpu.SemaphoreType.DMA((heads, 2)),
            pltpu.SemaphoreType.DMA((heads, 2)),
        ],
        compiler_params=pltpu.CompilerParams(
            collective_id=0, has_side_effects=True, vmem_limit_bytes=48 << 20
        ),
        cost_estimate=pl.CostEstimate(
            flops=12 * pairs * D, bytes_accessed=16 * rows * width, transcendentals=pairs
        ),
    )(queries, keys, values, out_grad, lengths.reshape(-1, 128))


def solution(mesh):
    spec = P("dp", "tensor")
    return jax.shard_map(
        body, mesh=mesh, in_specs=(spec,) * 4 + (P(),), out_specs=(spec,) * 4, check_vma=False
    )
```

time: 164 us -> 60.4 us (0.37)
  the two profiles are of different devices: /device:TPU:38 before, /device:TPU:6 now
where the time goes in v1:
time: 60.4 us; the launch traced here: 60.1 us
  Pallas kernels  51.8 us (86%)
  local copies, waits for them, and re-layouts  7.64 us (13%)
  between operations  0.65 us (1%)
    pallas_call x1, Pallas kernels, body(): pl.pallas_call(functools.partial(kernel, n_dp, rows, heads), out_shape=(o...  51.8 us
    unnamed x14, local copies, waits for them, and re-layouts  7.64 us

profile of v1, /device:TPU:6, one launch (start us, length us, event | category | flops | bytes accessed | tf_op | source)
XLA Modules:
  0.0 60.1 jit_solution(4540477673717983520)
XLA Ops:
  0.6 0.0 copy-start
  0.6 1.0 %copy-done = bf16[512,384]{1,0:T(8,128)(2,1)S(1)} copy-done((bf16[512,384]{1,0:T(8,128)(2,1)S(1)}, bf16[512,384]{1,0:T(8,128)(2,1)}, u32[]{:S(2)}) %copy-start) | copy-done | bytes 393240
  1.6 0.0 copy-start.1
  1.6 1.0 %copy-done.1 = bf16[512,384]{1,0:T(8,128)(2,1)S(1)} copy-done((bf16[512,384]{1,0:T(8,128)(2,1)S(1)}, bf16[512,384]{1,0:T(8,128)(2,1)}, u32[]{:S(2)}) %copy-start.1) | copy-done | bytes 393240
  2.6 0.0 copy-start.2
  2.6 1.0 %copy-done.2 = bf16[512,384]{1,0:T(8,128)(2,1)S(1)} copy-done((bf16[512,384]{1,0:T(8,128)(2,1)S(1)}, bf16[512,384]{1,0:T(8,128)(2,1)}, u32[]{:S(2)}) %copy-start.2) | copy-done | bytes 393240
  3.6 0.0 copy-start.3
  3.6 1.0 %copy-done.3 = bf16[512,384]{1,0:T(8,128)(2,1)S(1)} copy-done((bf16[512,384]{1,0:T(8,128)(2,1)S(1)}, bf16[512,384]{1,0:T(8,128)(2,1)}, u32[]{:S(2)}) %copy-start.3) | copy-done | bytes 393240
  4.6 0.0 copy-start.4
  4.6 0.7 %copy-done.4 = s32[384]{0:T(512)S(1)} copy-done((s32[384]{0:T(512)S(1)}, s32[384]{0:T(512)}, u32[]{:S(2)}) %copy-start.4) | copy-done | bytes 1560
  5.3 51.8 %shard_map.84 = (bf16[512,384]{1,0:T(8,128)(2,1)S(1)}, bf16[512,384]{1,0:T(8,128)(2,1)S(1)}, bf16[512,384]{1,0:T(8,128)(2,1)S(1)}, bf16[512,384]{1,0:T(8,128)(2,1)S(1)}) custom-call(bf16[512,384]{1,0:T(8,128)(2,1)S(1)} %copy-done, bf16[512,384]{1,0:T(8,128)(2,1)S(1)} %copy-done.1, bf16[512,384]{1,0:T(8,128)(2,1)S(1)} %copy-done.2, ...), custom_call_target="tpu_custom_call" | custom-call | flops 4831838208 | bytes 3145728 | tf_op jit(solution)/shard_map/pallas_call | solution.py:200
  57.1 0.7 %copy.13 = bf16[512,384]{1,0:T(8,128)(2,1)} copy(bf16[512,384]{1,0:T(8,128)(2,1)S(1)} %get-tuple-element.8) | data formatting | bytes 786432
  57.9 0.7 %copy.14 = bf16[512,384]{1,0:T(8,128)(2,1)} copy(bf16[512,384]{1,0:T(8,128)(2,1)S(1)} %get-tuple-element.9) | data formatting | bytes 786432
  58.6 0.7 %copy.15 = bf16[512,384]{1,0:T(8,128)(2,1)} copy(bf16[512,384]{1,0:T(8,128)(2,1)S(1)} %get-tuple-element.10) | data formatting | bytes 786432
  59.4 0.7 %copy.16 = bf16[512,384]{1,0:T(8,128)(2,1)} copy(bf16[512,384]{1,0:T(8,128)(2,1)S(1)} %get-tuple-element.11) | data formatting | bytes 786432
Async XLA Ops:
  0.6 1.0 %copy-start = (bf16[512,384]{1,0:T(8,128)(2,1)S(1)}, bf16[512,384]{1,0:T(8,128)(2,1)}, u32[]{:S(2)}) copy-start(bf16[512,384]{1,0:T(8,128)(2,1)} %q_hbm.1) | copy-start | bytes 1179652
  1.6 1.0 %copy-start.1 = (bf16[512,384]{1,0:T(8,128)(2,1)S(1)}, bf16[512,384]{1,0:T(8,128)(2,1)}, u32[]{:S(2)}) copy-start(bf16[512,384]{1,0:T(8,128)(2,1)} %k_hbm.1) | copy-start | bytes 1179652
  2.6 1.0 %copy-start.2 = (bf16[512,384]{1,0:T(8,128)(2,1)S(1)}, bf16[512,384]{1,0:T(8,128)(2,1)}, u32[]{:S(2)}) copy-start(bf16[512,384]{1,0:T(8,128)(2,1)} %v_hbm.1) | copy-start | bytes 1179652
  3.6 1.0 %copy-start.3 = (bf16[512,384]{1,0:T(8,128)(2,1)S(1)}, bf16[512,384]{1,0:T(8,128)(2,1)}, u32[]{:S(2)}) copy-start(bf16[512,384]{1,0:T(8,128)(2,1)} %g_hbm.1) | copy-start | bytes 1179652
  4.6 0.7 %copy-start.4 = (s32[384]{0:T(512)S(1)}, s32[384]{0:T(512)}, u32[]{:S(2)}) copy-start(s32[384]{0:T(512)} %param.9) | copy-start | bytes 4612

commit v2 on v1

--- a/solution.py
+++ b/solution.py
@@ -49,10 +49,10 @@
 
 def kernel(
     n_dp, rows, heads,
-    q_hbm, k_hbm, v_hbm, g_hbm, len_ref,
-    o_ref, dq_ref, dk_ref, dv_ref,
-    win, res, from_left, from_right, idc, idr, qt, gt, p_s, ds_s,
-    own_sem, send1, recv1, send2, recv2,
+    q_hbm, k_hbm, v_hbm, g_hbm, len_hbm,
+    out_ref,
+    win, res, from_left, from_right, idc, idr, qt, gt, p_s, ds_s, len_ref,
+    own_sem, len_sem, send1, recv1, send2, recv2,
 ):
     halo, d = HALO, D
     count = rows + 2 * halo
@@ -61,7 +61,7 @@
     right = lax.rem(me + 1, n_dp)
     left = lax.rem(me + n_dp - 1, n_dp)
     srcs = (q_hbm, k_hbm, v_hbm, g_hbm)
-    outs = (o_ref, dq_ref, dk_ref, dv_ref)
+    outs = tuple(out_ref.at[x] for x in range(4))
 
     def out_copy(x, h, way):
         cols = pl.ds(h * d, d)
@@ -97,6 +97,8 @@
             srcs[x].at[:, pl.ds(h * d, d)], win.at[x, h, pl.ds(halo, rows), :], own_sem.at[h, x]
         )
 
+    len_copy = pltpu.make_async_copy(len_hbm, len_ref, len_sem)
+    len_copy.start()
     barrier = pltpu.get_barrier_semaphore()
     for who in (left, right):
         pl.semaphore_signal(barrier, inc=1, device_id=(who, ten), device_id_type=MESH)
@@ -111,6 +113,7 @@
             own_copy(x, h).start()
 
     first = me * rows
+    len_copy.wait()
     begin, end = row_tables(len_ref, first, rows * n_dp, halo, rows)
     idc[...] = jnp.broadcast_to(begin, (count, d))
     idr[...] = jnp.transpose(jnp.broadcast_to(begin, (count, d)))[:8, :]
@@ -189,6 +192,15 @@
                 out_copy(x, h, way).wait_send()
 
 
+def store_kernel(o_in, dq_in, dk_in, dv_in, o, dq, dk, dv, sem):
+    pairs = ((o_in, o), (dq_in, dq), (dk_in, dk), (dv_in, dv))
+    copies = [pltpu.make_async_copy(a, b, sem.at[i]) for i, (a, b) in enumerate(pairs)]
+    for copy in copies:
+        copy.start()
+    for copy in copies:
+        copy.wait()
+
+
 def body(queries, keys, values, out_grad, lengths):
     rows, width = queries.shape
     heads = width // D
@@ -197,11 +209,15 @@
     out = jax.ShapeDtypeStruct((rows, width), jnp.bfloat16)
     bf = jnp.bfloat16
     pairs = count * count * heads
-    return pl.pallas_call(
+    operands = [
+        pltpu.with_memory_space_constraint(x, pltpu.MemorySpace.HBM)
+        for x in (queries, keys, values, out_grad, lengths.reshape(-1, 128))
+    ]
+    results = pl.pallas_call(
         functools.partial(kernel, n_dp, rows, heads),
-        out_shape=(out,) * 4,
-        in_specs=[pl.BlockSpec(memory_space=pl.ANY)] * 4 + [pl.BlockSpec(memory_space=pltpu.VMEM)],
-        out_specs=(pl.BlockSpec(memory_space=pltpu.VMEM),) * 4,
+        out_shape=jax.ShapeDtypeStruct((4, rows, width), jnp.bfloat16),
+        in_specs=[pl.BlockSpec(memory_space=pltpu.MemorySpace.HBM)] * 5,
+        out_specs=pl.BlockSpec(memory_space=pltpu.VMEM),
         scratch_shapes=[
             pltpu.VMEM((4, heads, count, D), bf),
             pltpu.VMEM((4, heads, count, D), bf),
@@ -213,7 +229,9 @@
             pltpu.VMEM((D, count), bf),
             pltpu.VMEM((count, count), bf),
             pltpu.VMEM((count, count), bf),
+            pltpu.VMEM((3, 128), jnp.int32),
             pltpu.SemaphoreType.DMA((heads, 4)),
+            pltpu.SemaphoreType.DMA(()),
             pltpu.SemaphoreType.DMA((heads, 4, 2)),
             pltpu.SemaphoreType.DMA((heads, 4, 2)),
             pltpu.SemaphoreType.DMA((heads, 2)),
@@ -225,7 +243,8 @@
         cost_estimate=pl.CostEstimate(
             flops=12 * pairs * D, bytes_accessed=16 * rows * width, transcendentals=pairs
         ),
-    )(queries, keys, values, out_grad, lengths.reshape(-1, 128))
+    )(*operands)
+    return tuple(results[x] for x in range(4))
 
 
 def solution(mesh):

time: 60.4 us -> 54 us (0.89)
  local copies, waits for them, and re-layouts: 7.64 us -> 1.18 us
    unnamed x14 -> x0, local copies, waits for them, and re-layouts: 7.64 us -> none
    squeeze x0 -> x1, local copies, waits for them, and re-layouts: none -> 1.18 us  [body(): return tuple((results[x] for x in range(4)))]
where the time goes in v2:
time: 54 us; the launch traced here: 53.9 us
  Pallas kernels  52 us (96%)
  local copies, waits for them, and re-layouts  1.18 us (2%)
  between operations  0.64 us (1%)
    pallas_call x1, Pallas kernels, body(): pl.pallas_call(functools.partial(kernel, n_dp, rows, heads), out_shape=ja...  52 us
    squeeze x1, local copies, waits for them, and re-layouts, body(): return tuple((results[x] for x in range(4)))  1.18 us

profile of v2, /device:TPU:6, one launch (start us, length us, event | category | flops | bytes accessed | tf_op | source)
XLA Modules:
  0.0 53.9 jit_solution(539630054065267823)
XLA Ops:
  0.6 52.0 %shard_map.84 = bf16[4,512,384]{2,1,0:T(8,128)(2,1)S(1)} custom-call(bf16[512,384]{1,0:T(8,128)(2,1)} %q_hbm.1, bf16[512,384]{1,0:T(8,128)(2,1)} %k_hbm.1, bf16[512,384]{1,0:T(8,128)(2,1)} %v_hbm.1, bf16[512,384]{1,0:T(8,128)(2,1)} %g_hbm.1, s32[3,128]{1,0:T(4,128)} %bitcast.9), custom_call_target="tpu_custom_call" | custom-call | flops 4831838208 | bytes 3145728 | tf_op jit(solution)/shard_map/pallas_call | solution.py:216
  52.7 1.2 %slice_bitcast_fusion = (bf16[512,384]{1,0:T(8,128)(2,1)}, bf16[512,384]{1,0:T(8,128)(2,1)}, bf16[512,384]{1,0:T(8,128)(2,1)}, bf16[512,384]{1,0:T(8,128)(2,1)}) fusion(bf16[4,512,384]{2,1,0:T(8,128)(2,1)S(1)} %shard_map.84), kind=kLoop, calls=%fused_computation | loop fusion | bytes 3145728 | tf_op jit(solution)/shard_map/squeeze | solution.py:247

commit v3 on v2

v3 whole, which is shorter than its diff:
```python
import functools
import math

import jax
import jax.numpy as jnp
from jax import lax
from jax.experimental import pallas as pl
from jax.experimental.pallas import tpu as pltpu
from jax.sharding import PartitionSpec as P

D = 128
EDGE = 128
HALO = 384
MESH = pl.DeviceIdType.MESH
LOG2E = 1.4426950408889634
BF = jnp.bfloat16
F32 = jnp.float32


def dot_nt(a, b):
    return lax.dot_general(a, b, (((1,), (1,)), ((), ())), preferred_element_type=F32)


def dot_nn(a, b):
    return jnp.dot(a, b, preferred_element_type=F32)


def row_tables(lens, first, count):
    upper = (
        lax.broadcasted_iota(jnp.int32, (128, 128), 0)
        <= lax.broadcasted_iota(jnp.int32, (128, 128), 1)
    ).astype(F32).astype(BF)
    high = (lens >> 4).astype(F32).astype(BF)
    low = (lens & 15).astype(F32).astype(BF)
    within = 16.0 * dot_nn(high, upper) + dot_nn(low, upper)
    pos = (first - HALO + lax.broadcasted_iota(jnp.int32, (count, 128), 0)).astype(F32)
    begin = jnp.zeros((count, 128), F32)
    end = jnp.full((count, 128), 1e9, F32)
    base = jnp.zeros((1, 1), F32)
    for g in range(lens.shape[0]):
        e = within[g : g + 1, :] + base
        base = base + within[g : g + 1, 127:128]
        past = e <= pos
        begin = jnp.maximum(begin, jnp.where(past, e, 0.0))
        end = jnp.minimum(end, jnp.where(past, 1e9, e))
    begin = jnp.max(begin, axis=1, keepdims=True)
    end = jnp.min(end, axis=1, keepdims=True)
    return jnp.where(pos[:, :1] < 0.0, -1.0, begin), end


def kernel(
    n_dp, rows, heads,
    q_hbm, k_hbm, v_hbm, g_hbm, len_hbm,
    out_ref,
    kv, q_own, g_own, qt, gt, packed, back, from_left, from_right,
    idc, idr, p_s, ds_s, own_kv, len_ref,
    own_sem, len_sem, send1, recv1, send2, recv2,
):
    halo, edge, d = HALO, EDGE, D
    count = rows + 2 * halo
    qrows = rows + 2 * edge
    me = lax.axis_index("dp")
    ten = lax.axis_index("tensor")
    right = lax.rem(me + 1, n_dp)
    left = lax.rem(me + n_dp - 1, n_dp)
    raw = halo - edge

    def remote(src, dst, send, recv, who):
        return pltpu.make_async_remote_copy(
            src_ref=src, dst_ref=dst, send_sem=send, recv_sem=recv,
            device_id=(who, ten), device_id_type=MESH,
        )

    def raw_copy(x, h, way):
        src = pl.ds(rows - raw, raw) if way == 0 else pl.ds(0, raw)
        dst = pl.ds(edge, raw) if way == 0 else pl.ds(halo + rows, raw)
        return remote(
            (k_hbm, v_hbm)[x].at[src, pl.ds(h * d, d)], kv.at[h, x, dst, :],
            send1.at[h, x, way], recv1.at[h, x, way], (right, left)[way],
        )

    def packed_copy(h, way):
        dst = pl.ds(0, edge) if way == 0 else pl.ds(count - edge, edge)
        return remote(
            packed.at[h, way], kv.at[h, :, dst, :],
            send1.at[h, 2, way], recv1.at[h, 2, way], (right, left)[way],
        )

    def back_copy(h, way):
        return remote(
            back.at[h, way], (from_left, from_right)[way].at[h],
            send2.at[h, way], recv2.at[h, way], (right, left)[way],
        )

    def own_copy(x, h):
        mid = pl.ds(halo, rows)
        dst = (q_own.at[h], kv.at[h, 0, mid, :], kv.at[h, 1, mid, :], g_own.at[h])[x]
        src = (q_hbm, k_hbm, v_hbm, g_hbm)[x]
        return pltpu.make_async_copy(src.at[:, pl.ds(h * d, d)], dst, own_sem.at[h, x])

    len_copy = pltpu.make_async_copy(len_hbm, len_ref, len_sem)
    len_copy.start()
    for h in range(heads):
        for x in range(4):
            own_copy(x, h).start()
    barrier = pltpu.get_barrier_semaphore()
    for who in (left, right):
        pl.semaphore_signal(barrier, inc=1, device_id=(who, ten), device_id_type=MESH)
    pl.semaphore_wait(barrier, 2)
    for way in range(2):
        for x in range(2):
            raw_copy(x, 0, way).start()

    first = me * rows
    len_copy.wait()
    begin, end = row_tables(len_ref[...], first, count)
    wide = jnp.broadcast_to(begin, (count, d))
    idc[...] = wide[halo - edge : halo + rows + edge]
    idr[...] = jnp.transpose(wide)[:8, :]
    lo = first.astype(F32)
    hi = (first + rows).astype(F32)
    b0, e0 = begin[halo : halo + 1], end[halo : halo + 1]
    spans_l = b0 < lo
    keep_l = spans_l & (e0 - lo > edge)
    moved_in_l = jnp.where(keep_l & (lo - b0 <= edge), 1.0, 0.0)
    shared_l = jnp.where(keep_l & (lo - b0 > edge), 1.0, 0.0)
    b1, e1 = begin[halo + rows - 1 : halo + rows], end[halo + rows - 1 : halo + rows]
    spans_r = e1 > hi
    moved_in_r = jnp.where(spans_r & (e1 - hi <= edge), 1.0, 0.0)
    far_r = spans_r & (e1 - hi > edge)
    moved_out_r = jnp.where(far_r & (hi - b1 <= edge), 1.0, 0.0)
    shared_r = jnp.where(far_r & (hi - b1 > edge), 1.0, 0.0)
    moved_out_l = jnp.where(spans_l & (e0 - lo <= edge), 1.0, 0.0)
    full = (edge, d)
    is_shared_l = jnp.broadcast_to(shared_l, full) > 0.5
    is_shared_r = jnp.broadcast_to(shared_r, full) > 0.5

    for h in range(heads):
        for x in range(4):
            own_copy(x, h).wait()
        if h > 0:
            for way in range(2):
                for x in range(2):
                    raw_copy(x, h, way).start()
        for x, own in ((0, q_own), (1, g_own)):
            packed[h, 0, x] = jnp.where(
                is_shared_r, kv[h, x, halo + rows - halo : halo + rows - raw, :],
                own[h, rows - edge : rows, :],
            )
            packed[h, 1, x] = jnp.where(
                is_shared_l, kv[h, x, halo + raw : halo + halo, :], own[h, 0:edge, :]
            )
        for way in range(2):
            packed_copy(h, way).start()
    for h in range(heads):
        qt[h, :, edge : edge + rows] = jnp.transpose(q_own[h])
        gt[h, :, edge : edge + rows] = jnp.transpose(g_own[h])

    factor = 1.0 / math.sqrt(d)
    last = count - edge
    half = rows // 2

    def one_head(h, carry):
        for way in range(2):
            for x in range(2):
                raw_copy(x, h, way).wait_recv()
            packed_copy(h, way).wait_recv()
        kv_q = (
            (kv[h, 0, 0:edge, :], kv[h, 1, 0:edge, :]),
            (q_own[h, 0:half, :], g_own[h, 0:half, :]),
            (q_own[h, half:rows, :], g_own[h, half:rows, :]),
            (kv[h, 0, last:count, :], kv[h, 1, last:count, :]),
        )
        qt[h, :, 0:edge] = jnp.transpose(kv_q[0][0])
        gt[h, :, 0:edge] = jnp.transpose(kv_q[0][1])
        qt[h, :, edge + rows :] = jnp.transpose(kv_q[3][0])
        gt[h, :, edge + rows :] = jnp.transpose(kv_q[3][1])
        spans = (
            (0, edge, halo - edge, halo + rows, moved_in_l),
            (edge, half, 0, count - edge, None),
            (edge + half, half, edge, count, None),
            (edge + rows, edge, halo, halo + rows + edge, moved_in_r),
        )
        outs = []
        for (qb, gb), (r0, n, k0, k1, valid) in zip(kv_q, spans):
            kb, vb = kv[h, 0, k0:k1, :], kv[h, 1, k0:k1, :]
            s = dot_nt(qb, kb) * (factor * LOG2E)
            s = jnp.where(idc[r0 : r0 + n, :1] == idr[:1, k0:k1], s, -1e30)
            top = jnp.max(s, axis=1, keepdims=True)
            w = jnp.exp2(s - top)
            total = jnp.sum(w, axis=1, keepdims=True)
            probs = w * ((1.0 if valid is None else valid) / total)
            low = probs.astype(BF)
            o = dot_nn(low, vb).astype(BF)
            p_s[r0 : r0 + n, k0:k1] = low
            gp = dot_nt(gb, vb)
            centre = jnp.sum(gb.astype(F32) * o.astype(F32), axis=1, keepdims=True)
            ds = (probs * (gp - centre)).astype(BF)
            ds_s[r0 : r0 + n, k0:k1] = ds
            dq = (dot_nn(ds, kb) * factor).astype(BF)
            outs.append((dq, o))

        def key_grads(r0, r1, c0, c1):
            dk = jnp.transpose(dot_nn(qt[h, :, r0:r1], ds_s[r0:r1, c0:c1]) * factor)
            dv = jnp.transpose(dot_nn(gt[h, :, r0:r1], p_s[r0:r1, c0:c1]))
            return dk, dv

        e, n = edge, qrows
        far = key_grads(e, e + half, 0, e)
        mid = key_grads(e, e + rows, e, 2 * e)
        near = key_grads(0, e + rows, 2 * e, 3 * e)
        for x in range(2):
            back[h, 1, x, 0:e] = jnp.where(is_shared_l, far[x].astype(BF), outs[0][x])
            back[h, 1, x, e : 2 * e] = mid[x].astype(BF)
            back[h, 1, x, 2 * e : 3 * e] = near[x].astype(BF)
        back_copy(h, 1).start()
        k = halo + rows
        near = key_grads(e, n, k, k + e)
        mid = key_grads(e, e + rows, k + e, k + 2 * e)
        far = key_grads(e + half, e + rows, k + 2 * e, k + 3 * e)
        for x in range(2):
            back[h, 0, x, 0:e] = near[x].astype(BF)
            back[h, 0, x, e : 2 * e] = mid[x].astype(BF)
            back[h, 0, x, 2 * e : 3 * e] = jnp.where(is_shared_r, far[x].astype(BF), outs[3][x])
        back_copy(h, 0).start()
        cols = pl.ds(pl.multiple_of(h * d, d), d)
        for i in range(2):
            rs = pl.ds(i * half, half)
            out_ref[1, rs, cols] = outs[1 + i][0]
            out_ref[0, rs, cols] = outs[1 + i][1]
            dk, dv = key_grads(0, n, halo + i * half, halo + (i + 1) * half)
            own_kv[h, 0, rs, :] = dk
            own_kv[h, 1, rs, :] = dv
        return carry

    lax.fori_loop(0, heads, one_head, 0)

    row_l = (begin[halo : halo + edge] < lo) & (jnp.broadcast_to(moved_out_l, (edge, 1)) > 0.5)
    row_r = (end[halo + rows - edge : halo + rows] > hi) & (
        jnp.broadcast_to(moved_out_r, (edge, 1)) > 0.5
    )
    full = (halo, d)
    add_l = jnp.broadcast_to(shared_l, full) > 0.5
    add_r = jnp.broadcast_to(shared_r, full) > 0.5
    tail = rows - edge
    for h in range(heads):
        for way in range(2):
            back_copy(h, way).wait_recv()
        cols = slice(h * d, (h + 1) * d)
        for x in range(2):
            fl = from_left[h, x].astype(F32)
            fr = from_right[h, x].astype(F32)
            out_ref[1 - x, 0:edge, cols] = jnp.where(
                row_l, from_left[h, x, 2 * edge :, :], out_ref[1 - x, 0:edge, cols]
            )
            out_ref[1 - x, tail:rows, cols] = jnp.where(
                row_r, from_right[h, x, 0:edge, :], out_ref[1 - x, tail:rows, cols]
            )
            own_kv[h, x, 0:halo, :] += jnp.where(add_l, fl, 0.0)
            own_kv[h, x, rows - halo : rows, :] += jnp.where(add_r, fr, 0.0)
            out_ref[2 + x, edge:tail, cols] = own_kv[h, x, edge:tail, :].astype(BF)
            out_ref[2 + x, 0:edge, cols] = jnp.where(
                row_l, fl[0:edge], own_kv[h, x, 0:edge, :]
            ).astype(BF)
            out_ref[2 + x, tail:rows, cols] = jnp.where(
                row_r, fr[2 * edge :], own_kv[h, x, tail:rows, :]
            ).astype(BF)
    for h in range(heads):
        for way in range(2):
            for x in range(2):
                raw_copy(x, h, way).wait_send()
            packed_copy(h, way).wait_send()
            back_copy(h, way).wait_send()


def body(queries, keys, values, out_grad, lengths):
    rows, width = queries.shape
    heads = width // D
    n_dp = lax.axis_size("dp")
    count = rows + 2 * HALO
    qrows = rows + 2 * EDGE
    pairs = qrows * count * heads
    operands = [
        pltpu.with_memory_space_constraint(x, pltpu.MemorySpace.HBM)
        for x in (queries, keys, values, out_grad, lengths.reshape(-1, 128))
    ]
    results = pl.pallas_call(
        functools.partial(kernel, n_dp, rows, heads),
        out_shape=jax.ShapeDtypeStruct((4, rows, width), BF),
        in_specs=[pl.BlockSpec(memory_space=pltpu.MemorySpace.HBM)] * 5,
        out_specs=pl.BlockSpec(memory_space=pltpu.VMEM),
        scratch_shapes=[
            pltpu.VMEM((heads, 2, count, D), BF),
            pltpu.VMEM((heads, rows, D), BF),
            pltpu.VMEM((heads, rows, D), BF),
            pltpu.VMEM((heads, D, qrows), BF),
            pltpu.VMEM((heads, D, qrows), BF),
            pltpu.VMEM((heads, 2, 2, EDGE, D), BF),
            pltpu.VMEM((heads, 2, 2, HALO, D), BF),
            pltpu.VMEM((heads, 2, HALO, D), BF),
            pltpu.VMEM((heads, 2, HALO, D), BF),
            pltpu.VMEM((qrows, D), F32),
            pltpu.VMEM((8, count), F32),
            pltpu.VMEM((qrows, count), BF),
            pltpu.VMEM((qrows, count), BF),
            pltpu.VMEM((heads, 2, rows, D), F32),
            pltpu.VMEM((lengths.shape[0] // 128, 128), jnp.int32),
            pltpu.SemaphoreType.DMA((heads, 4)),
            pltpu.SemaphoreType.DMA(()),
            pltpu.SemaphoreType.DMA((heads, 3, 2)),
            pltpu.SemaphoreType.DMA((heads, 3, 2)),
            pltpu.SemaphoreType.DMA((heads, 2)),
            pltpu.SemaphoreType.DMA((heads, 2)),
        ],
        compiler_params=pltpu.CompilerParams(
            collective_id=0, has_side_effects=True, vmem_limit_bytes=48 << 20
        ),
        cost_estimate=pl.CostEstimate(
            flops=12 * pairs * D, bytes_accessed=16 * rows * width, transcendentals=pairs
        ),
    )(*operands)
    return tuple(results[x] for x in range(4))


def solution(mesh):
    spec = P("dp", "tensor")
    return jax.shard_map(
        body, mesh=mesh, in_specs=(spec,) * 4 + (P(),), out_specs=(spec,) * 4, check_vma=False
    )
```

time: 54 us -> 48.5 us (0.90)
  Pallas kernels: 52 us -> 46.6 us
    pallas_call x1, Pallas kernels: 52 us -> 46.6 us  [body(): pl.pallas_call(functools.partial(kernel, n_dp, rows, heads), out_shape=ja...]
where the time goes in v3:
time: 48.5 us; the launch traced here: 48.4 us
  Pallas kernels  46.6 us (96%)
  local copies, waits for them, and re-layouts  1.18 us (2%)
  between operations  0.64 us (1%)
    pallas_call x1, Pallas kernels, body(): pl.pallas_call(functools.partial(kernel, n_dp, rows, heads), out_shape=ja...  46.6 us
    squeeze x1, local copies, waits for them, and re-layouts, body(): return tuple((results[x] for x in range(4)))  1.18 us

profile of v3, /device:TPU:6, one launch (start us, length us, event | category | flops | bytes accessed | tf_op | source)
XLA Modules:
  0.0 48.4 jit_solution(13396619859716978190)
XLA Ops:
  0.6 46.6 %shard_map.84 = bf16[4,512,384]{2,1,0:T(8,128)(2,1)S(1)} custom-call(bf16[512,384]{1,0:T(8,128)(2,1)} %q_hbm.1, bf16[512,384]{1,0:T(8,128)(2,1)} %k_hbm.1, bf16[512,384]{1,0:T(8,128)(2,1)} %v_hbm.1, bf16[512,384]{1,0:T(8,128)(2,1)} %g_hbm.1, s32[3,128]{1,0:T(4,128)} %bitcast.9), custom_call_target="tpu_custom_call" | custom-call | flops 4529848320 | bytes 3145728 | tf_op jit(solution)/shard_map/pallas_call | solution.py:287
  47.2 1.2 %slice_bitcast_fusion = (bf16[512,384]{1,0:T(8,128)(2,1)}, bf16[512,384]{1,0:T(8,128)(2,1)}, bf16[512,384]{1,0:T(8,128)(2,1)}, bf16[512,384]{1,0:T(8,128)(2,1)}) fusion(bf16[4,512,384]{2,1,0:T(8,128)(2,1)S(1)} %shard_map.84), kind=kLoop, calls=%fused_computation | loop fusion | bytes 3145728 | tf_op jit(solution)/shard_map/squeeze | solution.py:322

commit v4 on v3

--- a/solution.py
+++ b/solution.py
@@ -11,6 +11,7 @@
 D = 128
 EDGE = 128
 HALO = 384
+QBLK = 256
 MESH = pl.DeviceIdType.MESH
 LOG2E = 1.4426950408889634
 BF = jnp.bfloat16
@@ -54,7 +55,7 @@
     out_ref,
     kv, q_own, g_own, qt, gt, packed, back, from_left, from_right,
     idc, idr, p_s, ds_s, own_kv, len_ref,
-    own_sem, len_sem, send1, recv1, send2, recv2,
+    own_sem, len_sem, send1, recv1, send2, recv2, ready,
 ):
     halo, edge, d = HALO, EDGE, D
     count = rows + 2 * halo
@@ -63,6 +64,9 @@
     ten = lax.axis_index("tensor")
     right = lax.rem(me + 1, n_dp)
     left = lax.rem(me + n_dp - 1, n_dp)
+    has_left, has_right = me > 0, me < n_dp - 1
+    there = (has_right, has_left)
+    here = (has_left, has_right)
     raw = halo - edge
 
     def remote(src, dst, send, recv, who):
@@ -98,18 +102,34 @@
         src = (q_hbm, k_hbm, v_hbm, g_hbm)[x]
         return pltpu.make_async_copy(src.at[:, pl.ds(h * d, d)], dst, own_sem.at[h, x])
 
+    barrier = pltpu.get_barrier_semaphore()
+
+    @pl.when(has_left)
+    def _():
+        pl.semaphore_signal(barrier, inc=1, device_id=(left, ten), device_id_type=MESH)
+
     len_copy = pltpu.make_async_copy(len_hbm, len_ref, len_sem)
     len_copy.start()
     for h in range(heads):
         for x in range(4):
             own_copy(x, h).start()
-    barrier = pltpu.get_barrier_semaphore()
-    for who in (left, right):
-        pl.semaphore_signal(barrier, inc=1, device_id=(who, ten), device_id_type=MESH)
-    pl.semaphore_wait(barrier, 2)
-    for way in range(2):
+    @pl.when(has_right)
+    def _():
+        pl.semaphore_wait(barrier, 1)
+        pl.semaphore_signal(ready, inc=1, device_id=(right, ten), device_id_type=MESH)
         for x in range(2):
-            raw_copy(x, 0, way).start()
+            raw_copy(x, 0, 0).start()
+
+    @pl.when(jnp.logical_not(has_left))
+    def _():
+        kv[:, :, 0:halo, :] = jnp.zeros((heads, 2, halo, d), BF)
+        from_left[...] = jnp.zeros((heads, 2, halo, d), BF)
+
+    @pl.when(jnp.logical_not(has_right))
+    def _():
+        kv[:, :, halo + rows :, :] = jnp.zeros((heads, 2, halo, d), BF)
+        from_right[...] = jnp.zeros((heads, 2, halo, d), BF)
+
 
     first = me * rows
     len_copy.wait()
@@ -138,10 +158,6 @@
     for h in range(heads):
         for x in range(4):
             own_copy(x, h).wait()
-        if h > 0:
-            for way in range(2):
-                for x in range(2):
-                    raw_copy(x, h, way).start()
         for x, own in ((0, q_own), (1, g_own)):
             packed[h, 0, x] = jnp.where(
                 is_shared_r, kv[h, x, halo + rows - halo : halo + rows - raw, :],
@@ -150,8 +166,22 @@
             packed[h, 1, x] = jnp.where(
                 is_shared_l, kv[h, x, halo + raw : halo + halo, :], own[h, 0:edge, :]
             )
-        for way in range(2):
-            packed_copy(h, way).start()
+
+        @pl.when(has_right)
+        def _(h=h):
+            packed_copy(h, 0).start()
+            if h + 1 < heads:
+                for x in range(2):
+                    raw_copy(x, h + 1, 0).start()
+
+    @pl.when(has_left)
+    def _():
+        pl.semaphore_wait(ready, 1)
+        for h in range(heads):
+            for x in range(2):
+                raw_copy(x, h, 1).start()
+            packed_copy(h, 1).start()
+
     for h in range(heads):
         qt[h, :, edge : edge + rows] = jnp.transpose(q_own[h])
         gt[h, :, edge : edge + rows] = jnp.transpose(g_own[h])
@@ -160,29 +190,35 @@
     last = count - edge
     half = rows // 2
 
+    def key_grads(h, r0, r1, c0, c1):
+        dk = jnp.transpose(dot_nn(qt[h, :, r0:r1], ds_s[h, r0:r1, c0:c1]) * factor)
+        dv = jnp.transpose(dot_nn(gt[h, :, r0:r1], p_s[h, r0:r1, c0:c1]))
+        return dk, dv
+
     def one_head(h, carry):
         for way in range(2):
-            for x in range(2):
-                raw_copy(x, h, way).wait_recv()
-            packed_copy(h, way).wait_recv()
-        kv_q = (
-            (kv[h, 0, 0:edge, :], kv[h, 1, 0:edge, :]),
-            (q_own[h, 0:half, :], g_own[h, 0:half, :]),
-            (q_own[h, half:rows, :], g_own[h, half:rows, :]),
-            (kv[h, 0, last:count, :], kv[h, 1, last:count, :]),
-        )
-        qt[h, :, 0:edge] = jnp.transpose(kv_q[0][0])
-        gt[h, :, 0:edge] = jnp.transpose(kv_q[0][1])
-        qt[h, :, edge + rows :] = jnp.transpose(kv_q[3][0])
-        gt[h, :, edge + rows :] = jnp.transpose(kv_q[3][1])
-        spans = (
-            (0, edge, halo - edge, halo + rows, moved_in_l),
-            (edge, half, 0, count - edge, None),
-            (edge + half, half, edge, count, None),
-            (edge + rows, edge, halo, halo + rows + edge, moved_in_r),
-        )
+
+            @pl.when(here[way])
+            def _(way=way):
+                for x in range(2):
+                    raw_copy(x, h, way).wait_recv()
+                packed_copy(h, way).wait_recv()
+
+        low_q, low_g = kv[h, 0, 0:edge, :], kv[h, 1, 0:edge, :]
+        high_q, high_g = kv[h, 0, last:count, :], kv[h, 1, last:count, :]
+        qt[h, :, 0:edge] = jnp.transpose(low_q)
+        gt[h, :, 0:edge] = jnp.transpose(low_g)
+        qt[h, :, edge + rows :] = jnp.transpose(high_q)
+        gt[h, :, edge + rows :] = jnp.transpose(high_g)
+        blocks = [(low_q, low_g, 0, edge, halo - edge, halo + rows, moved_in_l)]
+        for r0 in range(0, rows, QBLK):
+            k0 = max(0, (r0 + 1 - rows + halo) // 128 * 128)
+            k1 = min(count, -(-(r0 + QBLK - 1 + rows + halo) // 128) * 128)
+            rs = slice(r0, r0 + QBLK)
+            blocks.append((q_own[h, rs, :], g_own[h, rs, :], edge + r0, QBLK, k0, k1, None))
+        blocks.append((high_q, high_g, edge + rows, edge, halo, halo + rows + edge, moved_in_r))
         outs = []
-        for (qb, gb), (r0, n, k0, k1, valid) in zip(kv_q, spans):
+        for qb, gb, r0, n, k0, k1, valid in blocks:
             kb, vb = kv[h, 0, k0:k1, :], kv[h, 1, k0:k1, :]
             s = dot_nt(qb, kb) * (factor * LOG2E)
             s = jnp.where(idc[r0 : r0 + n, :1] == idr[:1, k0:k1], s, -1e30)
@@ -192,48 +228,57 @@
             probs = w * ((1.0 if valid is None else valid) / total)
             low = probs.astype(BF)
             o = dot_nn(low, vb).astype(BF)
-            p_s[r0 : r0 + n, k0:k1] = low
+            p_s[h, r0 : r0 + n, k0:k1] = low
             gp = dot_nt(gb, vb)
             centre = jnp.sum(gb.astype(F32) * o.astype(F32), axis=1, keepdims=True)
             ds = (probs * (gp - centre)).astype(BF)
-            ds_s[r0 : r0 + n, k0:k1] = ds
+            ds_s[h, r0 : r0 + n, k0:k1] = ds
             dq = (dot_nn(ds, kb) * factor).astype(BF)
             outs.append((dq, o))
 
-        def key_grads(r0, r1, c0, c1):
-            dk = jnp.transpose(dot_nn(qt[h, :, r0:r1], ds_s[r0:r1, c0:c1]) * factor)
-            dv = jnp.transpose(dot_nn(gt[h, :, r0:r1], p_s[r0:r1, c0:c1]))
-            return dk, dv
-
-        e, n = edge, qrows
-        far = key_grads(e, e + half, 0, e)
-        mid = key_grads(e, e + rows, e, 2 * e)
-        near = key_grads(0, e + rows, 2 * e, 3 * e)
+        e, n, k = edge, qrows, halo + rows
+        near = key_grads(h, e, n, k, k + e)
+        mid = key_grads(h, e, e + rows, k + e, k + 2 * e)
+        far = key_grads(h, e + half, e + rows, k + 2 * e, k + 3 * e)
+        for x in range(2):
+            back[h, 0, x, 0:e] = near[x].astype(BF)
+            back[h, 0, x, e : 2 * e] = mid[x].astype(BF)
+            back[h, 0, x, 2 * e : 3 * e] = jnp.where(is_shared_r, far[x].astype(BF), outs[-1][x])
+
+        @pl.when(there[0])
+        def _():
+            back_copy(h, 0).start()
+
+        far = key_grads(h, e, e + half, 0, e)
+        mid = key_grads(h, e, e + rows, e, 2 * e)
+        near = key_grads(h, 0, e + rows, 2 * e, 3 * e)
         for x in range(2):
             back[h, 1, x, 0:e] = jnp.where(is_shared_l, far[x].astype(BF), outs[0][x])
             back[h, 1, x, e : 2 * e] = mid[x].astype(BF)
             back[h, 1, x, 2 * e : 3 * e] = near[x].astype(BF)
-        back_copy(h, 1).start()
-        k = halo + rows
-        near = key_grads(e, n, k, k + e)
-        mid = key_grads(e, e + rows, k + e, k + 2 * e)
-        far = key_grads(e + half, e + rows, k + 2 * e, k + 3 * e)
-        for x in range(2):
-            back[h, 0, x, 0:e] = near[x].astype(BF)
-            back[h, 0, x, e : 2 * e] = mid[x].astype(BF)
-            back[h, 0, x, 2 * e : 3 * e] = jnp.where(is_shared_r, far[x].astype(BF), outs[3][x])
-        back_copy(h, 0).start()
+
+        @pl.when(there[1])
+        def _():
+            back_copy(h, 1).start()
+
         cols = pl.ds(pl.multiple_of(h * d, d), d)
+        for i in range(rows // QBLK):
+            rs = pl.ds(i * QBLK, QBLK)
+            out_ref[1, rs, cols] = outs[1 + i][0]
+            out_ref[0, rs, cols] = outs[1 + i][1]
+        return carry
+
+    lax.fori_loop(0, heads, one_head, 0)
+
+    def own_key_grads(h, carry):
         for i in range(2):
             rs = pl.ds(i * half, half)
-            out_ref[1, rs, cols] = outs[1 + i][0]
-            out_ref[0, rs, cols] = outs[1 + i][1]
-            dk, dv = key_grads(0, n, halo + i * half, halo + (i + 1) * half)
+            dk, dv = key_grads(h, 0, qrows, halo + i * half, halo + (i + 1) * half)
             own_kv[h, 0, rs, :] = dk
             own_kv[h, 1, rs, :] = dv
         return carry
 
-    lax.fori_loop(0, heads, one_head, 0)
+    lax.fori_loop(0, heads, own_key_grads, 0)
 
     row_l = (begin[halo : halo + edge] < lo) & (jnp.broadcast_to(moved_out_l, (edge, 1)) > 0.5)
     row_r = (end[halo + rows - edge : halo + rows] > hi) & (
@@ -245,7 +290,11 @@
     tail = rows - edge
     for h in range(heads):
         for way in range(2):
-            back_copy(h, way).wait_recv()
+
+            @pl.when(here[way])
+            def _(h=h, way=way):
+                back_copy(h, way).wait_recv()
+
         cols = slice(h * d, (h + 1) * d)
         for x in range(2):
             fl = from_left[h, x].astype(F32)
@@ -267,10 +316,13 @@
             ).astype(BF)
     for h in range(heads):
         for way in range(2):
-            for x in range(2):
-                raw_copy(x, h, way).wait_send()
-            packed_copy(h, way).wait_send()
-            back_copy(h, way).wait_send()
+
+            @pl.when(there[way])
+            def _(h=h, way=way):
+                for x in range(2):
+                    raw_copy(x, h, way).wait_send()
+                packed_copy(h, way).wait_send()
+                back_copy(h, way).wait_send()
 
 
 def body(queries, keys, values, out_grad, lengths):
@@ -301,8 +353,8 @@
             pltpu.VMEM((heads, 2, HALO, D), BF),
             pltpu.VMEM((qrows, D), F32),
             pltpu.VMEM((8, count), F32),
-            pltpu.VMEM((qrows, count), BF),
-            pltpu.VMEM((qrows, count), BF),
+            pltpu.VMEM((heads, qrows, count), BF),
+            pltpu.VMEM((heads, qrows, count), BF),
             pltpu.VMEM((heads, 2, rows, D), F32),
             pltpu.VMEM((lengths.shape[0] // 128, 128), jnp.int32),
             pltpu.SemaphoreType.DMA((heads, 4)),
@@ -311,6 +363,7 @@
             pltpu.SemaphoreType.DMA((heads, 3, 2)),
             pltpu.SemaphoreType.DMA((heads, 2)),
             pltpu.SemaphoreType.DMA((heads, 2)),
+            pltpu.SemaphoreType.REGULAR,
         ],
         compiler_params=pltpu.CompilerParams(
             collective_id=0, has_side_effects=True, vmem_limit_bytes=48 << 20

time: 48.5 us -> 44.1 us (0.909)
  the two profiles are of different devices: /device:TPU:6 before, /device:TPU:38 now
where the time goes in v4:
time: 44.1 us; the launch traced here: 43.9 us
  Pallas kernels  42.1 us (95%)
  local copies, waits for them, and re-layouts  1.18 us (3%)
  between operations  0.64 us (1%)
    pallas_call x1, Pallas kernels, body(): pl.pallas_call(functools.partial(kernel, n_dp, rows, heads), out_shape=ja...  42.1 us
    squeeze x1, local copies, waits for them, and re-layouts, body(): return tuple((results[x] for x in range(4)))  1.18 us

profile of v4, /device:TPU:38, one launch (start us, length us, event | category | flops | bytes accessed | tf_op | source)
XLA Modules:
  0.0 43.9 jit_solution(4635830430128745647)
XLA Ops:
  0.6 42.1 %shard_map.84 = bf16[4,512,384]{2,1,0:T(8,128)(2,1)S(1)} custom-call(bf16[512,384]{1,0:T(8,128)(2,1)} %q_hbm.1, bf16[512,384]{1,0:T(8,128)(2,1)} %k_hbm.1, bf16[512,384]{1,0:T(8,128)(2,1)} %v_hbm.1, bf16[512,384]{1,0:T(8,128)(2,1)} %g_hbm.1, s32[3,128]{1,0:T(4,128)} %bitcast.9), custom_call_target="tpu_custom_call" | custom-call | flops 4529848320 | bytes 3145728 | tf_op jit(solution)/shard_map/pallas_call | solution.py:339
  42.8 1.2 %slice_bitcast_fusion = (bf16[512,384]{1,0:T(8,128)(2,1)}, bf16[512,384]{1,0:T(8,128)(2,1)}, bf16[512,384]{1,0:T(8,128)(2,1)}, bf16[512,384]{1,0:T(8,128)(2,1)}) fusion(bf16[4,512,384]{2,1,0:T(8,128)(2,1)S(1)} %shard_map.84), kind=kLoop, calls=%fused_computation | loop fusion | bytes 3145728 | tf_op jit(solution)/shard_map/squeeze | solution.py:375

commit v5 on v4

v5 whole, which is shorter than its diff:
```python
import functools
import math

import jax
import jax.numpy as jnp
from jax import lax
from jax.experimental import pallas as pl
from jax.experimental.pallas import tpu as pltpu
from jax.sharding import PartitionSpec as P

D = 128
EDGE_L, EDGE_R = 192, 128
HALO_L, HALO_R = 384, 320
PAD = 64
MESH = pl.DeviceIdType.MESH
LOG2E = 1.4426950408889634
BF = jnp.bfloat16
F32 = jnp.float32


def dot_nt(a, b):
    return lax.dot_general(a, b, (((1,), (1,)), ((), ())), preferred_element_type=F32)


def dot_nn(a, b):
    return jnp.dot(a, b, preferred_element_type=F32)


def row_tables(lens, first, count):
    upper = (
        lax.broadcasted_iota(jnp.int32, (128, 128), 0)
        <= lax.broadcasted_iota(jnp.int32, (128, 128), 1)
    ).astype(F32).astype(BF)
    high = (lens >> 4).astype(F32).astype(BF)
    low = (lens & 15).astype(F32).astype(BF)
    within = 16.0 * dot_nn(high, upper) + dot_nn(low, upper)
    pos = (first - HALO_L + lax.broadcasted_iota(jnp.int32, (count, 128), 0)).astype(F32)
    begin = jnp.zeros((count, 128), F32)
    end = jnp.full((count, 128), 1e9, F32)
    base = jnp.zeros((1, 1), F32)
    for g in range(lens.shape[0]):
        e = within[g : g + 1, :] + base
        base = base + within[g : g + 1, 127:128]
        past = e <= pos
        begin = jnp.maximum(begin, jnp.where(past, e, 0.0))
        end = jnp.minimum(end, jnp.where(past, 1e9, e))
    begin = jnp.max(begin, axis=1, keepdims=True)
    end = jnp.min(end, axis=1, keepdims=True)
    return jnp.where(pos[:, :1] < 0.0, -1.0, begin), end


def kernel(
    n_dp, rows, heads,
    q_hbm, k_hbm, v_hbm, g_hbm, len_hbm,
    out_ref,
    kv, q_own, g_own, qt, gt, packed_r, packed_l, back_r, back_l, from_left, from_right,
    idc, idr, p_s, ds_s, own_kv, len_ref,
    own_sem, len_sem, send1, recv1, send2, recv2, ready,
):
    hl, hr, el, er, d = HALO_L, HALO_R, EDGE_L, EDGE_R, D
    count = hl + rows + hr + PAD
    qrows = el + rows + er
    me = lax.axis_index("dp")
    ten = lax.axis_index("tensor")
    right = lax.rem(me + 1, n_dp)
    left = lax.rem(me + n_dp - 1, n_dp)
    has_left, has_right = me > 0, me < n_dp - 1
    there = (has_right, has_left)
    here = (has_left, has_right)
    raw = hl - el
    assert raw == hr - er

    def remote(src, dst, send, recv, who):
        return pltpu.make_async_remote_copy(
            src_ref=src, dst_ref=dst, send_sem=send, recv_sem=recv,
            device_id=(who, ten), device_id_type=MESH,
        )

    def raw_copy(x, h, way):
        src = pl.ds(rows - raw, raw) if way == 0 else pl.ds(0, raw)
        dst = pl.ds(el, raw) if way == 0 else pl.ds(hl + rows, raw)
        return remote(
            (k_hbm, v_hbm)[x].at[src, pl.ds(h * d, d)], kv.at[h, x, dst, :],
            send1.at[h, x, way], recv1.at[h, x, way], (right, left)[way],
        )

    def packed_copy(h, way):
        dst = pl.ds(0, el) if way == 0 else pl.ds(hl + rows + raw, er)
        return remote(
            (packed_r, packed_l)[way].at[h], kv.at[h, :, dst, :],
            send1.at[h, 2, way], recv1.at[h, 2, way], (right, left)[way],
        )

    def back_copy(h, way):
        return remote(
            (back_r, back_l)[way].at[h], (from_left, from_right)[way].at[h],
            send2.at[h, way], recv2.at[h, way], (right, left)[way],
        )

    def own_copy(x, h):
        mid = pl.ds(hl, rows)
        dst = (q_own.at[h], kv.at[h, 0, mid, :], kv.at[h, 1, mid, :], g_own.at[h])[x]
        src = (q_hbm, k_hbm, v_hbm, g_hbm)[x]
        return pltpu.make_async_copy(src.at[:, pl.ds(h * d, d)], dst, own_sem.at[h, x])

    barrier = pltpu.get_barrier_semaphore()

    @pl.when(has_left)
    def _():
        pl.semaphore_signal(barrier, inc=1, device_id=(left, ten), device_id_type=MESH)

    len_copy = pltpu.make_async_copy(len_hbm, len_ref, len_sem)
    len_copy.start()
    for h in range(heads):
        for x in range(4):
            own_copy(x, h).start()
    @pl.when(has_right)
    def _():
        pl.semaphore_wait(barrier, 1)
        pl.semaphore_signal(ready, inc=1, device_id=(right, ten), device_id_type=MESH)
        for x in range(2):
            raw_copy(x, 0, 0).start()

    @pl.when(jnp.logical_not(has_left))
    def _():
        kv[:, :, 0:hl, :] = jnp.zeros((heads, 2, hl, d), BF)
        from_left[...] = jnp.zeros((heads, 2, hr, d), BF)

    @pl.when(jnp.logical_not(has_right))
    def _():
        kv[:, :, hl + rows : hl + rows + hr, :] = jnp.zeros((heads, 2, hr, d), BF)
        from_right[...] = jnp.zeros((heads, 2, hl, d), BF)


    kv[:, :, count - PAD :, :] = jnp.zeros((heads, 2, PAD, d), BF)
    first = me * rows
    len_copy.wait()
    begin, end = row_tables(len_ref[...], first, count)
    wide = jnp.broadcast_to(begin, (count, d))
    idc[...] = wide[hl - el : hl + rows + er]
    idr[...] = jnp.transpose(wide)[:8, :]
    lo = first.astype(F32)
    hi = (first + rows).astype(F32)
    b0, e0 = begin[hl : hl + 1], end[hl : hl + 1]
    spans_l = b0 < lo
    keep_l = spans_l & (e0 - lo > er)
    moved_in_l = jnp.where(keep_l & (lo - b0 <= el), 1.0, 0.0)
    shared_l = jnp.where(keep_l & (lo - b0 > el), 1.0, 0.0)
    b1, e1 = begin[hl + rows - 1 : hl + rows], end[hl + rows - 1 : hl + rows]
    spans_r = e1 > hi
    moved_in_r = jnp.where(spans_r & (e1 - hi <= er), 1.0, 0.0)
    far_r = spans_r & (e1 - hi > er)
    moved_out_r = jnp.where(far_r & (hi - b1 <= el), 1.0, 0.0)
    shared_r = jnp.where(far_r & (hi - b1 > el), 1.0, 0.0)
    moved_out_l = jnp.where(spans_l & (e0 - lo <= er), 1.0, 0.0)

    def mask(flag, n):
        return jnp.broadcast_to(flag, (n, d)) > 0.5


    for h in range(heads):
        for x in range(4):
            own_copy(x, h).wait()
        for x, own in ((0, q_own), (1, g_own)):
            packed_r[h, x] = jnp.where(
                mask(shared_r, el), kv[h, x, rows : rows + el, :], own[h, rows - el : rows, :]
            )
            packed_l[h, x] = jnp.where(
                mask(shared_l, er), kv[h, x, hl + raw : hl + raw + er, :], own[h, 0:er, :]
            )

        @pl.when(has_right)
        def _(h=h):
            packed_copy(h, 0).start()
            if h + 1 < heads:
                for x in range(2):
                    raw_copy(x, h + 1, 0).start()

    @pl.when(has_left)
    def _():
        pl.semaphore_wait(ready, 1)
        for h in range(heads):
            for x in range(2):
                raw_copy(x, h, 1).start()
            packed_copy(h, 1).start()

    for h in range(heads):
        qt[h, :, 0:rows] = jnp.transpose(q_own[h])
        gt[h, :, 0:rows] = jnp.transpose(g_own[h])

    factor = 1.0 / math.sqrt(d)
    half = rows // 2
    k = hl + rows
    low, high = slice(0, el), slice(k + raw, k + raw + er)

    def query_block(h, qb, gb, r0, n, k0, k1, valid):
        kb, vb = kv[h, 0, k0:k1, :], kv[h, 1, k0:k1, :]
        s = dot_nt(qb, kb) * (factor * LOG2E)
        s = jnp.where(idc[r0 : r0 + n, :1] == idr[:1, k0:k1], s, -1e30)
        top = jnp.max(s, axis=1, keepdims=True)
        w = jnp.exp2(s - top)
        total = jnp.sum(w, axis=1, keepdims=True)
        probs = w * ((1.0 if valid is None else valid) / total)
        p = probs.astype(BF)
        o = dot_nn(p, vb).astype(BF)
        p_s[h, r0 : r0 + n, k0:k1] = p
        gp = dot_nt(gb, vb)
        centre = jnp.sum(gb.astype(F32) * o.astype(F32), axis=1, keepdims=True)
        ds = (probs * (gp - centre)).astype(BF)
        ds_s[h, r0 : r0 + n, k0:k1] = ds
        return (dot_nn(ds, kb) * factor).astype(BF), o

    def key_grads(h, c0, c1, own=(0, rows), from_low=False, from_high=False):
        cs = slice(c0, c1)
        rs = slice(el + own[0], el + own[1])
        dk = dot_nn(qt[h, :, own[0] : own[1]], ds_s[h, rs, cs])
        dv = dot_nn(gt[h, :, own[0] : own[1]], p_s[h, rs, cs])
        if from_high:
            rs = slice(el + rows, qrows)
            dk += dot_nn(qt[h, :, rows : rows + er], ds_s[h, rs, cs])
            dv += dot_nn(gt[h, :, rows : rows + er], p_s[h, rs, cs])
        if from_low:
            rs, ts = slice(0, el), slice(rows + er, rows + er + el)
            dk += dot_nn(qt[h, :, ts], ds_s[h, rs, cs])
            dv += dot_nn(gt[h, :, ts], p_s[h, rs, cs])
        return jnp.transpose(dk * factor), jnp.transpose(dv)

    def right_side(h, carry):
        for way in range(2):

            @pl.when(here[way])
            def _(way=way):
                for x in range(2):
                    raw_copy(x, h, way).wait_recv()
                packed_copy(h, way).wait_recv()

        cols = pl.ds(pl.multiple_of(h * d, d), d)
        for r0 in range(0, rows, half):
            k0 = max(0, (r0 + 1 - rows + hl) // 128 * 128)
            k1 = min(count, -(-(r0 + half - 1 + rows + hl) // 128) * 128)
            rs = slice(r0, r0 + half)
            dq, o = query_block(h, q_own[h, rs, :], g_own[h, rs, :], el + r0, half, k0, k1, None)
            out_ref[1, rs, cols] = dq
            out_ref[0, rs, cols] = o
        qb, gb = kv[h, 0, high, :], kv[h, 1, high, :]
        qt[h, :, rows : rows + er] = jnp.transpose(qb)
        gt[h, :, rows : rows + er] = jnp.transpose(gb)
        moved = query_block(h, qb, gb, el + rows, er, hl, k + er, moved_in_r)
        near = key_grads(h, k, k + 128, from_high=True)
        mid = key_grads(h, k + 128, k + 256)
        far = key_grads(h, k + 256, k + 384, own=(half, rows))
        for x in range(2):
            back_r[h, x, 0:128] = near[x].astype(BF)
            back_r[h, x, 128:raw] = mid[x][0 : raw - 128].astype(BF)
            tail = jnp.concatenate([mid[x][raw - 128 :], far[x][0 : hr - 256]], axis=0)
            back_r[h, x, raw:hr] = jnp.where(mask(shared_r, er), tail.astype(BF), moved[x])

        @pl.when(has_right)
        def _():
            back_copy(h, 0).start()

        return carry


    def left_side(h, carry):
        qb, gb = kv[h, 0, low, :], kv[h, 1, low, :]
        qt[h, :, rows + er : rows + er + el] = jnp.transpose(qb)
        gt[h, :, rows + er : rows + er + el] = jnp.transpose(gb)
        moved = query_block(h, qb, gb, 0, el, hl - 256, k, moved_in_l)
        far = key_grads(h, 0, 128, own=(0, half))
        mid = key_grads(h, 128, 256, from_low=True)
        near = key_grads(h, 256, 384, from_low=True)
        for x in range(2):
            head = jnp.concatenate([far[x], mid[x][0 : el - 128]], axis=0)
            back_l[h, x, 0:el] = jnp.where(mask(shared_l, el), head.astype(BF), moved[x])
            back_l[h, x, el:256] = mid[x][el - 128 :].astype(BF)
            back_l[h, x, 256:hl] = near[x].astype(BF)

        @pl.when(has_left)
        def _():
            back_copy(h, 1).start()

        return carry

    lax.fori_loop(0, heads, lambda h, c: left_side(h, right_side(h, c)), 0)

    def own_key_grads(h, carry):
        for i in range(2):
            rs = pl.ds(i * half, half)
            own_kv[h, 0, rs, :], own_kv[h, 1, rs, :] = key_grads(
                h, hl + i * half, hl + (i + 1) * half, from_low=True, from_high=True
            )
        return carry

    lax.fori_loop(0, heads, own_key_grads, 0)

    row_l = (begin[hl : hl + er] < lo) & (jnp.broadcast_to(moved_out_l, (er, 1)) > 0.5)
    row_r = (end[k - el : k] > hi) & (jnp.broadcast_to(moved_out_r, (el, 1)) > 0.5)
    add_l, add_r = mask(shared_l, hr), mask(shared_r, hl)
    tail = rows - el
    for h in range(heads):
        for way in range(2):

            @pl.when(here[way])
            def _(h=h, way=way):
                back_copy(h, way).wait_recv()

        cols = slice(h * d, (h + 1) * d)
        for x in range(2):
            fl = from_left[h, x].astype(F32)
            fr = from_right[h, x].astype(F32)
            out_ref[1 - x, 0:er, cols] = jnp.where(
                row_l, from_left[h, x, raw:hr, :], out_ref[1 - x, 0:er, cols]
            )
            out_ref[1 - x, tail:rows, cols] = jnp.where(
                row_r, from_right[h, x, 0:el, :], out_ref[1 - x, tail:rows, cols]
            )
            own_kv[h, x, 0:hr, :] += jnp.where(add_l, fl, 0.0)
            own_kv[h, x, rows - hl : rows, :] += jnp.where(add_r, fr, 0.0)
            out_ref[2 + x, er:tail, cols] = own_kv[h, x, er:tail, :].astype(BF)
            out_ref[2 + x, 0:er, cols] = jnp.where(
                row_l, fl[0:er], own_kv[h, x, 0:er, :]
            ).astype(BF)
            out_ref[2 + x, tail:rows, cols] = jnp.where(
                row_r, fr[hl - el :], own_kv[h, x, tail:rows, :]
            ).astype(BF)
    for h in range(heads):
        for way in range(2):

            @pl.when(there[way])
            def _(h=h, way=way):
                for x in range(2):
                    raw_copy(x, h, way).wait_send()
                packed_copy(h, way).wait_send()
                back_copy(h, way).wait_send()


def body(queries, keys, values, out_grad, lengths):
    rows, width = queries.shape
    heads = width // D
    n_dp = lax.axis_size("dp")
    count = HALO_L + rows + HALO_R + PAD
    qrows = EDGE_L + rows + EDGE_R
    pairs = qrows * count * heads
    operands = [
        pltpu.with_memory_space_constraint(x, pltpu.MemorySpace.HBM)
        for x in (queries, keys, values, out_grad, lengths.reshape(-1, 128))
    ]
    results = pl.pallas_call(
        functools.partial(kernel, n_dp, rows, heads),
        out_shape=jax.ShapeDtypeStruct((4, rows, width), BF),
        in_specs=[pl.BlockSpec(memory_space=pltpu.MemorySpace.HBM)] * 5,
        out_specs=pl.BlockSpec(memory_space=pltpu.VMEM),
        scratch_shapes=[
            pltpu.VMEM((heads, 2, count, D), BF),
            pltpu.VMEM((heads, rows, D), BF),
            pltpu.VMEM((heads, rows, D), BF),
            pltpu.VMEM((heads, D, qrows), BF),
            pltpu.VMEM((heads, D, qrows), BF),
            pltpu.VMEM((heads, 2, EDGE_L, D), BF),
            pltpu.VMEM((heads, 2, EDGE_R, D), BF),
            pltpu.VMEM((heads, 2, HALO_R, D), BF),
            pltpu.VMEM((heads, 2, HALO_L, D), BF),
            pltpu.VMEM((heads, 2, HALO_R, D), BF),
            pltpu.VMEM((heads, 2, HALO_L, D), BF),
            pltpu.VMEM((qrows, D), F32),
            pltpu.VMEM((8, count), F32),
            pltpu.VMEM((heads, qrows, count), BF),
            pltpu.VMEM((heads, qrows, count), BF),
            pltpu.VMEM((heads, 2, rows, D), F32),
            pltpu.VMEM((lengths.shape[0] // 128, 128), jnp.int32),
            pltpu.SemaphoreType.DMA((heads, 4)),
            pltpu.SemaphoreType.DMA(()),
            pltpu.SemaphoreType.DMA((heads, 3, 2)),
            pltpu.SemaphoreType.DMA((heads, 3, 2)),
            pltpu.SemaphoreType.DMA((heads, 2)),
            pltpu.SemaphoreType.DMA((heads, 2)),
            pltpu.SemaphoreType.REGULAR,
        ],
        compiler_params=pltpu.CompilerParams(
            collective_id=0, has_side_effects=True, vmem_limit_bytes=48 << 20
        ),
        cost_estimate=pl.CostEstimate(
            flops=12 * pairs * D, bytes_accessed=16 * rows * width, transcendentals=pairs
        ),
    )(*operands)
    return tuple(results[x] for x in range(4))


def solution(mesh):
    spec = P("dp", "tensor")
    return jax.shard_map(
        body, mesh=mesh, in_specs=(spec,) * 4 + (P(),), out_specs=(spec,) * 4, check_vma=False
    )
```

time: 44.1 us -> 42.8 us (0.971)
  Pallas kernels: 42.1 us -> 40.8 us
    pallas_call x1, Pallas kernels: 42.1 us -> 40.8 us  [body(): pl.pallas_call(functools.partial(kernel, n_dp, rows, heads), out_shape=ja...]
where the time goes in v5:
time: 42.8 us; the launch traced here: 42.6 us
  Pallas kernels  40.8 us (95%)
  local copies, waits for them, and re-layouts  1.18 us (3%)
  between operations  0.64 us (1%)
    pallas_call x1, Pallas kernels, body(): pl.pallas_call(functools.partial(kernel, n_dp, rows, heads), out_shape=ja...  40.8 us
    squeeze x1, local copies, waits for them, and re-layouts, body(): return tuple((results[x] for x in range(4)))  1.18 us

profile of v5, /device:TPU:38, one launch (start us, length us, event | category | flops | bytes accessed | tf_op | source)
XLA Modules:
  0.0 42.6 jit_solution(15408519849666766118)
XLA Ops:
  0.6 40.8 %shard_map.84 = bf16[4,512,384]{2,1,0:T(8,128)(2,1)S(1)} custom-call(bf16[512,384]{1,0:T(8,128)(2,1)} %q_hbm.1, bf16[512,384]{1,0:T(8,128)(2,1)} %k_hbm.1, bf16[512,384]{1,0:T(8,128)(2,1)} %v_hbm.1, bf16[512,384]{1,0:T(8,128)(2,1)} %g_hbm.1, s32[3,128]{1,0:T(4,128)} %bitcast.9), custom_call_target="tpu_custom_call" | custom-call | flops 4907335680 | bytes 3145728 | tf_op jit(solution)/shard_map/pallas_call | solution.py:349
  41.4 1.2 %slice_bitcast_fusion = (bf16[512,384]{1,0:T(8,128)(2,1)}, bf16[512,384]{1,0:T(8,128)(2,1)}, bf16[512,384]{1,0:T(8,128)(2,1)}, bf16[512,384]{1,0:T(8,128)(2,1)}) fusion(bf16[4,512,384]{2,1,0:T(8,128)(2,1)S(1)} %shard_map.84), kind=kLoop, calls=%fused_computation | loop fusion | bytes 3145728 | tf_op jit(solution)/shard_map/squeeze | solution.py:387

commit v6 on v5

--- a/solution.py
+++ b/solution.py
@@ -235,11 +235,9 @@
                 packed_copy(h, way).wait_recv()
 
         cols = pl.ds(pl.multiple_of(h * d, d), d)
-        for r0 in range(0, rows, half):
-            k0 = max(0, (r0 + 1 - rows + hl) // 128 * 128)
-            k1 = min(count, -(-(r0 + half - 1 + rows + hl) // 128) * 128)
-            rs = slice(r0, r0 + half)
-            dq, o = query_block(h, q_own[h, rs, :], g_own[h, rs, :], el + r0, half, k0, k1, None)
+        for r0 in range(0, rows, rows):
+            rs = slice(0, rows)
+            dq, o = query_block(h, q_own[h], g_own[h], el, rows, 0, count, None)
             out_ref[1, rs, cols] = dq
             out_ref[0, rs, cols] = o
         qb, gb = kv[h, 0, high, :], kv[h, 1, high, :]

time: 42.8 us -> 42.1 us (0.984)
  Pallas kernels: 40.8 us -> 40.1 us
    pallas_call x1, Pallas kernels: 40.8 us -> 40.1 us  [body(): pl.pallas_call(functools.partial(kernel, n_dp, rows, heads), out_shape=ja...]
where the time goes in v6:
time: 42.1 us; the launch traced here: 41.9 us
  Pallas kernels  40.1 us (95%)
  local copies, waits for them, and re-layouts  1.18 us (3%)
  between operations  0.64 us (2%)
    pallas_call x1, Pallas kernels, body(): pl.pallas_call(functools.partial(kernel, n_dp, rows, heads), out_shape=ja...  40.1 us
    squeeze x1, local copies, waits for them, and re-layouts, body(): return tuple((results[x] for x in range(4)))  1.18 us

profile of v6, /device:TPU:38, one launch (start us, length us, event | category | flops | bytes accessed | tf_op | source)
XLA Modules:
  0.0 41.9 jit_solution(17967282903414103613)
XLA Ops:
  0.6 40.1 %shard_map.84 = bf16[4,512,384]{2,1,0:T(8,128)(2,1)S(1)} custom-call(bf16[512,384]{1,0:T(8,128)(2,1)} %q_hbm.1, bf16[512,384]{1,0:T(8,128)(2,1)} %k_hbm.1, bf16[512,384]{1,0:T(8,128)(2,1)} %v_hbm.1, bf16[512,384]{1,0:T(8,128)(2,1)} %g_hbm.1, s32[3,128]{1,0:T(4,128)} %bitcast.9), custom_call_target="tpu_custom_call" | custom-call | flops 4907335680 | bytes 3145728 | tf_op jit(solution)/shard_map/pallas_call | solution.py:347
  40.7 1.2 %slice_bitcast_fusion = (bf16[512,384]{1,0:T(8,128)(2,1)}, bf16[512,384]{1,0:T(8,128)(2,1)}, bf16[512,384]{1,0:T(8,128)(2,1)}, bf16[512,384]{1,0:T(8,128)(2,1)}) fusion(bf16[4,512,384]{2,1,0:T(8,128)(2,1)S(1)} %shard_map.84), kind=kLoop, calls=%fused_computation | loop fusion | bytes 3145728 | tf_op jit(solution)/shard_map/squeeze | solution.py:385

commit v7 on v6

--- a/solution.py
+++ b/solution.py
@@ -210,7 +210,7 @@
         ds_s[h, r0 : r0 + n, k0:k1] = ds
         return (dot_nn(ds, kb) * factor).astype(BF), o
 
-    def key_grads(h, c0, c1, own=(0, rows), from_low=False, from_high=False):
+    def key_grads(h, c0, c1, own=(0, rows), from_low=False, from_high=False, kind=BF):
         cs = slice(c0, c1)
         rs = slice(el + own[0], el + own[1])
         dk = dot_nn(qt[h, :, own[0] : own[1]], ds_s[h, rs, cs])
@@ -223,7 +223,7 @@
             rs, ts = slice(0, el), slice(rows + er, rows + er + el)
             dk += dot_nn(qt[h, :, ts], ds_s[h, rs, cs])
             dv += dot_nn(gt[h, :, ts], p_s[h, rs, cs])
-        return jnp.transpose(dk * factor), jnp.transpose(dv)
+        return jnp.transpose((dk * factor).astype(kind)), jnp.transpose(dv.astype(kind))
 
     def right_side(h, carry):
         for way in range(2):
@@ -248,10 +248,10 @@
         mid = key_grads(h, k + 128, k + 256)
         far = key_grads(h, k + 256, k + 384, own=(half, rows))
         for x in range(2):
-            back_r[h, x, 0:128] = near[x].astype(BF)
-            back_r[h, x, 128:raw] = mid[x][0 : raw - 128].astype(BF)
+            back_r[h, x, 0:128] = near[x]
+            back_r[h, x, 128:raw] = mid[x][0 : raw - 128]
             tail = jnp.concatenate([mid[x][raw - 128 :], far[x][0 : hr - 256]], axis=0)
-            back_r[h, x, raw:hr] = jnp.where(mask(shared_r, er), tail.astype(BF), moved[x])
+            back_r[h, x, raw:hr] = jnp.where(mask(shared_r, er), tail, moved[x])
 
         @pl.when(has_right)
         def _():
@@ -270,9 +270,9 @@
         near = key_grads(h, 256, 384, from_low=True)
         for x in range(2):
             head = jnp.concatenate([far[x], mid[x][0 : el - 128]], axis=0)
-            back_l[h, x, 0:el] = jnp.where(mask(shared_l, el), head.astype(BF), moved[x])
-            back_l[h, x, el:256] = mid[x][el - 128 :].astype(BF)
-            back_l[h, x, 256:hl] = near[x].astype(BF)
+            back_l[h, x, 0:el] = jnp.where(mask(shared_l, el), head, moved[x])
+            back_l[h, x, el:256] = mid[x][el - 128 :]
+            back_l[h, x, 256:hl] = near[x]
 
         @pl.when(has_left)
         def _():
@@ -286,7 +286,7 @@
         for i in range(2):
             rs = pl.ds(i * half, half)
             own_kv[h, 0, rs, :], own_kv[h, 1, rs, :] = key_grads(
-                h, hl + i * half, hl + (i + 1) * half, from_low=True, from_high=True
+                h, hl + i * half, hl + (i + 1) * half, from_low=True, from_high=True, kind=F32
             )
         return carry
 

time: 42.1 us -> 42 us (level)
  no operation moved by 1% of the time
where the time goes in v7:
time: 42 us; the launch traced here: 41.9 us
  Pallas kernels  40 us (95%)
  local copies, waits for them, and re-layouts  1.18 us (3%)
  between operations  0.64 us (2%)
    pallas_call x1, Pallas kernels, body(): pl.pallas_call(functools.partial(kernel, n_dp, rows, heads), out_shape=ja...  40 us
    squeeze x1, local copies, waits for them, and re-layouts, body(): return tuple((results[x] for x in range(4)))  1.18 us

profile of v7, /device:TPU:38, one launch (start us, length us, event | category | flops | bytes accessed | tf_op | source)
XLA Modules:
  0.0 41.9 jit_solution(3693680850847173368)
XLA Ops:
  0.6 40.0 %shard_map.84 = bf16[4,512,384]{2,1,0:T(8,128)(2,1)S(1)} custom-call(bf16[512,384]{1,0:T(8,128)(2,1)} %q_hbm.1, bf16[512,384]{1,0:T(8,128)(2,1)} %k_hbm.1, bf16[512,384]{1,0:T(8,128)(2,1)} %v_hbm.1, bf16[512,384]{1,0:T(8,128)(2,1)} %g_hbm.1, s32[3,128]{1,0:T(4,128)} %bitcast.9), custom_call_target="tpu_custom_call" | custom-call | flops 4907335680 | bytes 3145728 | tf_op jit(solution)/shard_map/pallas_call | solution.py:347
  40.7 1.2 %slice_bitcast_fusion = (bf16[512,384]{1,0:T(8,128)(2,1)}, bf16[512,384]{1,0:T(8,128)(2,1)}, bf16[512,384]{1,0:T(8,128)(2,1)}, bf16[512,384]{1,0:T(8,128)(2,1)}) fusion(bf16[4,512,384]{2,1,0:T(8,128)(2,1)S(1)} %shard_map.84), kind=kLoop, calls=%fused_computation | loop fusion | bytes 3145728 | tf_op jit(solution)/shard_map/squeeze | solution.py:385
